TPU v7x, 512 devices: a whole 4x4x16 slice. The times are simulated.
512 devices in a mesh: shard: 16 (over z), group: 32 (over x, y, core).
Axes of the slice: x: 4, y: 4, z: 16, core: 2. Of those that a mesh axis runs over, the one named last changes fastest.
Arguments:
- momentum: bfloat16 [512, 1024, 512], P('group', 'shard'), may hold values from -40 to 40
- gradient: bfloat16 [512, 1024, 512], P('group', 'shard'), may hold values from -300 to 300
- weights: bfloat16 [512, 1024, 512], P('group', 'shard'), may hold values from -0.1875 to 0.1875
- slot_map: int32 [32, 16], P('group'), may hold values from 0 to 7, as said below
- tokens: bfloat16 [16, 32, 256, 1024], P('shard', 'group'), may hold values from -6 to 6
Outputs:
- fresh_state: bfloat16 [512, 1024, 512], P('group', 'shard')
- hidden: bfloat16 [16, 32, 256, 512], P('shard', 'group')
Inputs may be any that keep to these rules, and one draw needn't show every extreme that they name: `slot_map`: each row holds every expert-layer of its group at least once and at most four times.
All inputs are finite; a program needn't handle non-finite values.
Results may differ from a plain program's by a relative error of at most 0.014.
Values may be sent and summed in bfloat16 or wider, within the bound.
No kernel may reach another device: no remote copies, remote signals or barrier semaphores. Data moves between devices by JAX's collectives and lax.ppermute only.
A program may use at most 64 MiB of HBM per device.

v0:
```python
import math

import jax
import jax.numpy as jnp
from jax import lax
from jax.sharding import Mesh
from jax.sharding import PartitionSpec as P

D = 1024
F = 512
ITERS = 5
GROUP = ("group_0", "group_1", "group_2")
SHARD_GROUP = ("shard", "group_0", "group_1", "group_2")


coefficients = (3.4445, -4.775, 2.0315)
momentum_decay = 0.95
learning_rate = 0.05
clip_rms = 0.5


def one_axis_at_a_time(x, axes):
    for axis in axes:
        x = lax.psum(x, axis)
    return x


def in_blocks(x, dim, peers):
    before, after = (x.shape[:dim], x.shape[dim + 1 :])
    return jnp.moveaxis(x.reshape(*before, peers, -1, *after), dim, 0)


def edges_of(length, count):
    unit = 8 if length >= 8 * count else 1
    return [length // unit * k // count * unit for k in range(1, count)]


def in_order(tiles, dim):
    tiles = jnp.moveaxis(tiles, 0, dim)
    dims = tiles.shape
    return tiles.reshape(*dims[:dim], dims[dim] * dims[dim + 1], *dims[dim + 2 :])


def exchange_in_pieces(x, axis, pieces, split_dim, concat_dim):
    tiles = in_blocks(x, split_dim, lax.axis_size(axis))
    cut = max(range(1, max(2, tiles.ndim - 1)), key=lambda d: tiles.shape[d])
    done = []
    for slab in jnp.split(tiles, edges_of(tiles.shape[cut], pieces), axis=cut):
        if slab.size:
            done.append(lax.all_to_all(slab, axis, split_axis=0, concat_axis=0, tiled=True))
    return in_order(jnp.concatenate(done, axis=cut), concat_dim)


def orthogonal(matrix):
    widened = matrix.astype(jnp.float32)
    inverse_norm = 1.0 / (jnp.sqrt(jnp.sum(widened * widened)) + 1e-07)
    iterate = (widened * inverse_norm).astype(jnp.bfloat16)
    for iteration in range(ITERS):
        gram = lax.dot_general(
            iterate, iterate, (((0,), (0,)), ((), ())), preferred_element_type=jnp.float32
        ).astype(jnp.bfloat16)
        squared = jnp.dot(gram, gram, preferred_element_type=jnp.float32)
        polynomial = (
            coefficients[1] * gram.astype(jnp.float32) + coefficients[2] * squared
        ).astype(jnp.bfloat16)
        product = jnp.dot(iterate, polynomial, preferred_element_type=jnp.float32)
        iterate = (coefficients[0] * iterate.astype(jnp.float32) + product).astype(jnp.bfloat16)
    return (0.2 * math.sqrt(D) * iterate.astype(jnp.float32)).astype(jnp.bfloat16)


def local(momentum, gradient, weights, slot_map, tokens):
    owners = lax.axis_size("shard")
    every_entry = owners * lax.axis_size(GROUP) * D * F
    widened = gradient.astype(jnp.float32)
    grand_total = one_axis_at_a_time(jnp.sum(widened * widened), SHARD_GROUP)
    clip_factor = jnp.minimum(
        1.0, clip_rms * math.sqrt(every_entry) / jnp.sqrt(grand_total + 1e-06)
    )
    fresh_state = (momentum_decay * momentum.astype(jnp.float32) + clip_factor * widened).astype(
        jnp.bfloat16
    )
    mixed = lax.all_to_all(fresh_state, "shard", split_axis=0, concat_axis=1, tiled=True)[0]
    update = orthogonal(mixed)
    update_rows = exchange_in_pieces(update[None], "shard", 2, 1, 0)
    new_weights = (
        weights.astype(jnp.float32) - learning_rate * update_rows.astype(jnp.float32)
    ).astype(jnp.bfloat16)
    paired = new_weights.reshape(owners // 2, 2, new_weights.shape[1], new_weights.shape[2])
    picked = jnp.take(paired, slot_map[0], axis=0)
    slot_pair = lax.all_to_all(picked, "shard", split_axis=0, concat_axis=2, tiled=True)[0]
    prompt = tokens[0, 0]
    gate_out = jnp.dot(prompt, slot_pair[0], preferred_element_type=jnp.float32)
    up_out = jnp.dot(prompt, slot_pair[1], preferred_element_type=jnp.float32)
    hidden = (jax.nn.silu(gate_out) * up_out).astype(jnp.bfloat16)
    return (fresh_state, hidden[None, None])


def solution(mesh):
    split = Mesh(
        mesh.devices.reshape(mesh.shape["shard"], 4, 4, 2),
        ("shard", "group_0", "group_1", "group_2"),
    )
    placed = (
        P(GROUP, "shard", None),
        P(GROUP, "shard", None),
        P(GROUP, "shard", None),
        P(GROUP, None),
        P("shard", GROUP, None, None),
    )
    return jax.shard_map(
        local,
        mesh=split,
        in_specs=placed,
        out_specs=(P(GROUP, "shard", None), P("shard", GROUP, None, None)),
        check_vma=False,
    )
```

profile of v0, /device:TPU:32, one launch (start us, length us, event | category | flops | bytes accessed | tf_op | source)
XLA Modules:
  0.0 321.2 jit_solution(6416869554844856845)
XLA Ops:
  0.6 0.0 copy-start
  0.6 2.4 fusion
  3.1 35.0 %psum.28 = f32[]{:T(128)} all-reduce(f32[]{:T(128)} %fusion), channel_id=1, replica_groups=mesh['shard'=16,'group_0'=4,'group_1'=4,'group_2'=2] {'shard'}, use_global_device_ids=true, to_apply=%region_1.0 | all-reduce | flops 1 | bytes 8 | tf_op jit(solution)/shard_map/psum | solution.py:24
  38.1 11.1 %psum.29 = f32[]{:T(128)} all-reduce(f32[]{:T(128)} %psum.28), channel_id=1, replica_groups=mesh['shard'=16,'group_0'=4,'group_1'=4,'group_2'=2] {'group_0'}, use_global_device_ids=true, to_apply=%region_2.0 | all-reduce | flops 1 | bytes 8 | tf_op jit(solution)/shard_map/psum | solution.py:24
  49.2 11.3 %psum.30 = f32[]{:T(128)} all-reduce(f32[]{:T(128)} %psum.29), channel_id=1, replica_groups=mesh['shard'=16,'group_0'=4,'group_1'=4,'group_2'=2] {'group_1'}, use_global_device_ids=true, to_apply=%region_3.0 | all-reduce | flops 1 | bytes 8 | tf_op jit(solution)/shard_map/psum | solution.py:24
  60.5 3.1 psum.31
  64.3 1.9 fusion.2
  66.2 0.0 copy-start.1
  66.2 60.6 %all_to_all.34 = bf16[16,64,512]{2,1,0:T(8,128)(2,1)S(1)} all-to-all(bf16[16,64,512]{2,1,0:T(8,128)(2,1)S(1)} %fusion.2), channel_id=1, replica_groups=mesh['shard'=16,'group_0'=4,'group_1'=4,'group_2'=2] {'shard'}, dimensions={0} | all-to-all | bytes 2097152 | tf_op jit(solution)/shard_map/all_to_all | solution.py:82
  126.8 1.1 fusion.3
  128.7 0.2 fusion.4
  128.9 0.0 copy-done.1
  128.9 0.0 copy-start.2
  128.9 0.7 fusion.11
  129.6 0.2 copy-done.2
  129.9 2.6 add_convert_fusion.4
  132.5 0.7 convolution_convert_fusion.3
  133.2 1.1 add_convert_fusion.3
  134.3 0.7 convolution_convert_fusion.2
  135.0 1.1 add_convert_fusion.2
  136.1 0.7 convolution_convert_fusion.1
  136.8 1.1 add_convert_fusion.1
  137.9 0.7 convolution_convert_fusion
  138.6 1.1 multiply_convert_fusion
  139.7 0.0 copy-start.3
  139.7 0.9 fusion.54
  140.6 34.9 %all_to_all.35 = bf16[16,1,32,512]{3,2,1,0:T(8,128)(2,1)S(1)} all-to-all(bf16[16,1,32,512]{3,2,1,0:T(8,128)(2,1)S(1)} %get-tuple-element.8), channel_id=1, replica_groups=mesh['shard'=16,'group_0'=4,'group_1'=4,'group_2'=2] {'shard'}, dimensions={0} | all-to-all | bytes 1048576 | tf_op jit(solution)/shard_map/all_to_all | solution.py:50
  175.5 6.8 %all-to-all-start.2 = ((bf16[16,1,32,512]{3,2,1,0:T(8,128)(2,1)}), bf16[16,1,32,512]{3,2,1,0:T(8,128)(2,1)S(1)}, u32[]{:S(2)}, u32[]{:S(2)}) async-start(bf16[16,1,32,512]{3,2,1,0:T(8,128)(2,1)} %get-tuple-element.9), calls=%async_computation.2 | async-start | bytes 1048576 | tf_op jit(solution)/shard_map/all_to_all | solution.py:50
  182.3 0.0 copy-done.3
  182.3 28.7 %all-to-all-done.2 = bf16[16,1,32,512]{3,2,1,0:T(8,128)(2,1)S(1)} async-done(((bf16[16,1,32,512]{3,2,1,0:T(8,128)(2,1)}), bf16[16,1,32,512]{3,2,1,0:T(8,128)(2,1)S(1)}, u32[]{:S(2)}, u32[]{:S(2)}) %all-to-all-start.2) | async-done | bytes 524320 | tf_op jit(solution)/shard_map/all_to_all | solution.py:50
  211.1 1.6 fusion.5
  212.6 2.0 gather_fusion
  214.7 1.9 broadcast_select_fusion
  216.5 102.6 %all_to_all.36 = bf16[16,2,64,512]{3,2,1,0:T(8,128)(2,1)S(1)} all-to-all(bf16[16,2,64,512]{3,2,1,0:T(8,128)(2,1)S(1)} %broadcast_select_fusion), channel_id=1, replica_groups=mesh['shard'=16,'group_0'=4,'group_1'=4,'group_2'=2] {'shard'}, dimensions={0} | all-to-all | bytes 4194304 | tf_op jit(solution)/shard_map/all_to_all | solution.py:90
  319.1 0.2 fusion.53
  319.4 0.0 copy-done
  319.4 0.5 convolution_bitcast_fusion.2
  319.9 0.5 fusion.19
  320.4 0.8 copy.10
  (3 shorter events, 0.0 us)
Async XLA Ops:
  0.6 318.7 %copy-start = (bf16[1,1,256,1024]{3,2,1,0:T(8,128)(2,1)S(1)}, bf16[1,1,256,1024]{3,2,1,0:T(8,128)(2,1)}, u32[]{:S(2)}) copy-start(bf16[1,1,256,1024]{3,2,1,0:T(8,128)(2,1)} %param.9) | copy-start | bytes 1572868
  66.2 62.7 %copy-start.1 = (bf16[16,64,512]{2,1,0:T(8,128)(2,1)}, bf16[16,64,512]{2,1,0:T(8,128)(2,1)S(1)}, u32[]{:S(2)}) copy-start(bf16[16,64,512]{2,1,0:T(8,128)(2,1)S(1)} %fusion.2) | copy-start | bytes 3145732
  128.9 1.0 copy-start.2
  139.7 42.5 %copy-start.3 = (s32[1,16]{1,0:T(1,128)S(1)}, s32[1,16]{1,0:T(1,128)}, u32[]{:S(2)}) copy-start(s32[1,16]{1,0:T(1,128)} %param.8) | copy-start | bytes 196
  175.5 35.6 %all-to-all-start.2 = ((bf16[16,1,32,512]{3,2,1,0:T(8,128)(2,1)}), bf16[16,1,32,512]{3,2,1,0:T(8,128)(2,1)S(1)}, u32[]{:S(2)}, u32[]{:S(2)}) async-start(bf16[16,1,32,512]{3,2,1,0:T(8,128)(2,1)} %get-tuple-element.9), calls=%async_computation.2 | async-start | bytes 1048576 | tf_op jit(solution)/shard_map/all_to_all | solution.py:50
where the time goes:
time: 322 us; the launch traced here: 321 us
  blocking collectives  259 us (80%)
  waiting for transfers between devices  28.7 us (9%)
  matrix products  11.5 us (4%)
  other arithmetic  9.14 us (3%)
  starting transfers between devices  6.79 us (2%)
  local copies, waits for them, and re-layouts  4.23 us (1%)
    all_to_all x1, blocking collectives, local(): lax.all_to_all(picked, 'shard', split_axis=0, concat_axis=2, tiled=True)[0]  103 us
    all_to_all x1, blocking collectives, local(): lax.all_to_all(fresh_state, 'shard', split_axis=0, concat_axis=1, tiled=T...  60.6 us
    psum x4, blocking collectives, one_axis_at_a_time(): x = lax.psum(x, axis)  60.5 us
    all_to_all x1, blocking collectives, exchange_in_pieces(): lax.all_to_all(slab, axis, split_axis=0, concat_axis=0, tiled=True)  34.9 us
    all_to_all x1, waiting for transfers between devices, exchange_in_pieces(): lax.all_to_all(slab, axis, split_axis=0, concat_axis=0, tiled=True)  28.7 us
    dot_general x5, matrix products, orthogonal(): product = jnp.dot(iterate, polynomial, preferred_element_type=jnp.float32)  6.84 us
    all_to_all x1, starting transfers between devices, exchange_in_pieces(): lax.all_to_all(slab, axis, split_axis=0, concat_axis=0, tiled=True)  6.79 us
  transfers between devices with their start and end apart: 1, of which 1 were waited for; matrix products, arithmetic and copies ran while one was open for 0% of the time, Pallas kernels for 0%

commit v1 on v0

v1 whole, which is shorter than its diff:
```python
import math

import jax
import jax.numpy as jnp
from jax import lax
from jax.sharding import Mesh
from jax.sharding import PartitionSpec as P

D = 1024
F = 512
ITERS = 5
GROUP = ("group_0", "group_1", "group_2")

coefficients = (3.4445, -4.775, 2.0315)
momentum_decay = 0.95
learning_rate = 0.05
clip_rms = 0.5


def spread(x):
    return lax.all_to_all(x, "shard", split_axis=0, concat_axis=0, tiled=True)


def total_over(value, axes):
    peers = math.prod(lax.axis_size(axis) for axis in axes)
    mine = jnp.broadcast_to(value, (peers, 8, 128))
    theirs = lax.all_to_all(mine, axes, split_axis=0, concat_axis=0, tiled=True)
    return jnp.sum(theirs[:, 0, 0])


def orthogonal(matrix):
    widened = matrix.astype(jnp.float32)
    inverse_norm = 1.0 / (jnp.sqrt(jnp.sum(widened * widened)) + 1e-07)
    iterate = (widened * inverse_norm).astype(jnp.bfloat16)
    for iteration in range(ITERS):
        gram = lax.dot_general(
            iterate, iterate, (((0,), (0,)), ((), ())), preferred_element_type=jnp.float32
        ).astype(jnp.bfloat16)
        squared = jnp.dot(gram, gram, preferred_element_type=jnp.float32)
        polynomial = (
            coefficients[1] * gram.astype(jnp.float32) + coefficients[2] * squared
        ).astype(jnp.bfloat16)
        product = jnp.dot(iterate, polynomial, preferred_element_type=jnp.float32)
        iterate = (coefficients[0] * iterate.astype(jnp.float32) + product).astype(jnp.bfloat16)
    return (0.2 * math.sqrt(D) * iterate.astype(jnp.float32)).astype(jnp.bfloat16)


def stepped(weights, update):
    return (weights.astype(jnp.float32) - learning_rate * update.astype(jnp.float32)).astype(
        jnp.bfloat16
    )


def local(momentum, gradient, weights, slot_map, tokens):
    owners = lax.axis_size("shard")
    every_entry = owners * lax.axis_size(GROUP) * D * F
    rows = weights.shape[1]
    chosen = 2 * slot_map[0]

    def of_slots(x, k):
        return x.at[chosen + k].get(mode="promise_in_bounds")

    old_gate = spread(of_slots(weights, 0)).reshape(D, F)
    widened = gradient.astype(jnp.float32)
    grand_total = total_over(total_over(jnp.sum(widened * widened), ("shard",)), GROUP)
    clip_factor = jnp.minimum(
        1.0, clip_rms * math.sqrt(every_entry) / jnp.sqrt(grand_total + 1e-06)
    )
    fresh_state = (momentum_decay * momentum.astype(jnp.float32) + clip_factor * widened).astype(
        jnp.bfloat16
    )
    state_gate = spread(of_slots(fresh_state, 0)).reshape(D, F)
    state_up = spread(of_slots(fresh_state, 1)).reshape(D, F)
    old_up = spread(of_slots(weights, 1)).reshape(D, F)
    prompt = tokens[0, 0]
    new_gate = stepped(old_gate, orthogonal(state_gate))
    gate_out = jnp.dot(prompt, new_gate, preferred_element_type=jnp.float32)
    new_up = stepped(old_up, orthogonal(state_up))
    up_out = jnp.dot(prompt, new_up, preferred_element_type=jnp.float32)
    hidden = (jax.nn.silu(gate_out) * up_out).astype(jnp.bfloat16)
    return (fresh_state, hidden[None, None])


def solution(mesh):
    split = Mesh(
        mesh.devices.reshape(mesh.shape["shard"], 4, 4, 2),
        ("shard", "group_0", "group_1", "group_2"),
    )
    placed = (
        P(GROUP, "shard", None),
        P(GROUP, "shard", None),
        P(GROUP, "shard", None),
        P(GROUP, None),
        P("shard", GROUP, None, None),
    )
    return jax.shard_map(
        local,
        mesh=split,
        in_specs=placed,
        out_specs=(P(GROUP, "shard", None), P("shard", GROUP, None, None)),
        check_vma=False,
    )
```

time: 322 us -> 288 us (0.89)
  blocking collectives: 259 us -> 26.5 us
  waiting for transfers between devices: 28.7 us -> 151 us
  matrix products: 11.5 us -> 51.7 us
  starting transfers between devices: 6.79 us -> 37 us
  local copies, waits for them, and re-layouts: 4.23 us -> 10.2 us
    all_to_all x3 -> x1, blocking collectives: 198 us -> 26.5 us  [total_over(): theirs = lax.all_to_all(mine, axes, split_axis=0, concat_axis=0, tiled=True)]
    all_to_all x1 -> x5, waiting for transfers between devices: 28.7 us -> 151 us  [the longest x4 143 us: spread(): return lax.all_to_all(x, 'shard', split_axis=0, concat_axis=0, tiled=True)]
    psum x4 -> x0, blocking collectives: 60.5 us -> none  [one_axis_at_a_time(): x = lax.psum(x, axis)]
    all_to_all x1 -> x5, starting transfers between devices: 6.79 us -> 37 us  [the longest x4 29.7 us: spread(): return lax.all_to_all(x, 'shard', split_axis=0, concat_axis=0, tiled=True)]
    dot_general x5 -> x9, matrix products: 6.84 us -> 28.1 us  [orthogonal(): product = jnp.dot(iterate, polynomial, preferred_element_type=jnp.float32)]
    dot_general x5 -> x10, matrix products: 3.69 us -> 17 us  [orthogonal(): lax.dot_general(iterate, iterate, (((0,), (0,)), ((), ())), preferred_ele...]
    dot_general x2 -> x3, matrix products: 0.97 us -> 6.56 us  [the longest x1 3.47 us: local(): gate_out = jnp.dot(prompt, new_gate, preferred_element_type=jnp.float32)]
    gather x1 -> x4, local copies, waits for them, and re-layouts: 2.03 us -> 6.4 us  [of_slots(): return x.at[chosen + k].get(mode='promise_in_bounds')]
  transfers between devices with their start and end apart: 1 -> 5, of which waited for: 1 -> 5; matrix products, arithmetic and copies ran while one was open for 0% -> 19% of each run, Pallas kernels for 0% -> 0%
where the time goes in v1:
time: 288 us; the launch traced here: 287 us
  waiting for transfers between devices  151 us (52%)
  matrix products  51.7 us (18%)
  starting transfers between devices  37 us (13%)
  blocking collectives  26.5 us (9%)
  local copies, waits for them, and re-layouts  10.2 us (4%)
  other arithmetic  8.07 us (3%)
  between operations  3.03 us (1%)
    all_to_all x4, waiting for transfers between devices, spread(): return lax.all_to_all(x, 'shard', split_axis=0, concat_axis=0, tiled=True)  143 us
    all_to_all x4, starting transfers between devices, spread(): return lax.all_to_all(x, 'shard', split_axis=0, concat_axis=0, tiled=True)  29.7 us
    dot_general x9, matrix products, orthogonal(): product = jnp.dot(iterate, polynomial, preferred_element_type=jnp.float32)  28.1 us
    all_to_all x1, blocking collectives, total_over(): theirs = lax.all_to_all(mine, axes, split_axis=0, concat_axis=0, tiled=True)  26.5 us
    dot_general x10, matrix products, orthogonal(): lax.dot_general(iterate, iterate, (((0,), (0,)), ((), ())), preferred_ele...  17 us
    all_to_all x1, waiting for transfers between devices, total_over(): theirs = lax.all_to_all(mine, axes, split_axis=0, concat_axis=0, tiled=True)  7.8 us
    all_to_all x1, starting transfers between devices, total_over(): theirs = lax.all_to_all(mine, axes, split_axis=0, concat_axis=0, tiled=True)  7.32 us
    gather x4, local copies, waits for them, and re-layouts, of_slots(): return x.at[chosen + k].get(mode='promise_in_bounds')  6.4 us
  transfers between devices with their start and end apart: 5, of which 5 were waited for; matrix products, arithmetic and copies ran while one was open for 19% of the time, Pallas kernels for 0%

profile of v1, /device:TPU:32, one launch (start us, length us, event | category | flops | bytes accessed | tf_op | source)
XLA Modules:
  0.0 287.5 jit_solution(14479259714530845755)
XLA Ops:
  0.7 2.5 fusion
  3.2 0.6 broadcast_in_dim.6
  3.8 26.5 %all_to_all.30 = f32[16,8,128]{2,1,0:T(8,128)S(1)} all-to-all(f32[16,8,128]{2,1,0:T(8,128)S(1)} %broadcast_in_dim.6), channel_id=1, replica_groups=mesh['shard'=16,'group_0'=4,'group_1'=4,'group_2'=2] {'shard'}, dimensions={0} | all-to-all | bytes 131072 | tf_op jit(solution)/shard_map/all_to_all | solution.py:27
  30.4 0.6 slice_reduce_fusion.1
  31.0 1.3 broadcast_in_dim.14
  32.3 7.3 %all-to-all-start.1 = ((f32[32,8,128]{2,1,0:T(8,128)}), f32[32,8,128]{2,1,0:T(8,128)S(1)}, u32[]{:S(2)}, u32[]{:S(2)}) async-start(f32[32,8,128]{2,1,0:T(8,128)} %broadcast_in_dim.14), calls=%async_computation.1 | async-start | bytes 262144 | tf_op jit(solution)/shard_map/all_to_all | solution.py:27
  39.7 7.8 %all-to-all-done.1 = f32[32,8,128]{2,1,0:T(8,128)S(1)} async-done(((f32[32,8,128]{2,1,0:T(8,128)}), f32[32,8,128]{2,1,0:T(8,128)S(1)}, u32[]{:S(2)}, u32[]{:S(2)}) %all-to-all-start.1) | async-done | bytes 131104 | tf_op jit(solution)/shard_map/all_to_all | solution.py:27
  47.5 0.6 slice_reduce_fusion
  48.8 1.6 fusion.2
  50.4 1.6 gather_fusion.1
  52.1 4.7 %all-to-all-start.3 = ((bf16[16,64,512]{2,1,0:T(8,128)(2,1)}), bf16[16,64,512]{2,1,0:T(8,128)(2,1)S(1)}, u32[]{:S(2)}, u32[]{:S(2)}) async-start(bf16[16,64,512]{2,1,0:T(8,128)(2,1)} %gather_fusion.1), calls=%async_computation.3 | async-start | bytes 2097152 | tf_op jit(solution)/shard_map/all_to_all | solution.py:21
  56.8 1.6 gather_fusion.3
  58.4 48.7 %all-to-all-done.3 = bf16[16,64,512]{2,1,0:T(8,128)(2,1)S(1)} async-done(((bf16[16,64,512]{2,1,0:T(8,128)(2,1)}), bf16[16,64,512]{2,1,0:T(8,128)(2,1)S(1)}, u32[]{:S(2)}, u32[]{:S(2)}) %all-to-all-start.3) | async-done | bytes 1048608 | tf_op jit(solution)/shard_map/all_to_all | solution.py:21
  107.1 8.2 %all-to-all-start.5 = ((bf16[16,64,512]{2,1,0:T(8,128)(2,1)}), bf16[16,64,512]{2,1,0:T(8,128)(2,1)S(1)}, u32[]{:S(2)}, u32[]{:S(2)}) async-start(bf16[16,64,512]{2,1,0:T(8,128)(2,1)} %gather_fusion.3), calls=%async_computation.5 | async-start | bytes 2097152 | tf_op jit(solution)/shard_map/all_to_all | solution.py:21
  115.3 1.6 gather_fusion.2
  116.9 48.1 %all-to-all-done.5 = bf16[16,64,512]{2,1,0:T(8,128)(2,1)S(1)} async-done(((bf16[16,64,512]{2,1,0:T(8,128)(2,1)}), bf16[16,64,512]{2,1,0:T(8,128)(2,1)S(1)}, u32[]{:S(2)}, u32[]{:S(2)}) %all-to-all-start.5) | async-done | bytes 1048608 | tf_op jit(solution)/shard_map/all_to_all | solution.py:21
  165.0 8.3 %all-to-all-start.4 = ((bf16[16,64,512]{2,1,0:T(8,128)(2,1)}), bf16[16,64,512]{2,1,0:T(8,128)(2,1)}, u32[]{:S(2)}, u32[]{:S(2)}) async-start(bf16[16,64,512]{2,1,0:T(8,128)(2,1)} %gather_fusion.2), calls=%async_computation.4 | async-start | bytes 2097152 | tf_op jit(solution)/shard_map/all_to_all | solution.py:21
  173.3 1.6 gather_fusion
  174.9 1.1 fusion.3
  176.8 1.1 fusion.5
  178.7 0.2 fusion.4
  178.9 1.6 fusion.19
  180.4 3.2 %add_convert_fusion.9 = bf16[1024,512]{1,0:T(8,128)(2,1)S(1)} fusion(bf16[1024,512]{1,0:T(8,128)(2,1)} %bitcast.95, bf16[512,512]{1,0:T(8,128)(2,1)} %fusion.19), kind=kOutput, calls=%fused_computation.32 | convolution fusion | flops 808714240 | bytes 2621440 | tf_op jit(solution)/shard_map/dot_general | solution.py:43
  183.6 1.6 convolution_convert_fusion.7
  185.2 3.5 %add_convert_fusion.8 = bf16[1024,512]{1,0:T(8,128)(2,1)} fusion(bf16[1024,512]{1,0:T(8,128)(2,1)S(1)} %add_convert_fusion.9, bf16[512,512]{1,0:T(8,128)(2,1)} %convolution_convert_fusion.7), kind=kOutput, calls=%fused_computation.31 | convolution fusion | flops 808714240 | bytes 2621440 | tf_op jit(solution)/shard_map/dot_general | solution.py:43
  188.7 3.2 %convolution_convert_fusion.6 = bf16[512,512]{1,0:T(8,128)(2,1)} fusion(bf16[1024,512]{1,0:T(8,128)(2,1)} %add_convert_fusion.8), kind=kOutput, calls=%fused_computation.73 | convolution fusion | flops 537133056 | bytes 1572864 | tf_op jit(solution)/shard_map/dot_general | solution.py:36
  191.8 3.5 %add_convert_fusion.7 = bf16[1024,512]{1,0:T(8,128)(2,1)} fusion(bf16[1024,512]{1,0:T(8,128)(2,1)S(1)} %copy-done.10, bf16[512,512]{1,0:T(8,128)(2,1)} %convolution_convert_fusion.6), kind=kOutput, calls=%fused_computation.30 | convolution fusion | flops 808714240 | bytes 2621440 | tf_op jit(solution)/shard_map/dot_general | solution.py:43
  195.3 3.1 %convolution_convert_fusion.5 = bf16[512,512]{1,0:T(8,128)(2,1)} fusion(bf16[1024,512]{1,0:T(8,128)(2,1)} %add_convert_fusion.7), kind=kOutput, calls=%fused_computation.72 | convolution fusion | flops 537133056 | bytes 1572864 | tf_op jit(solution)/shard_map/dot_general | solution.py:36
  198.4 3.2 %add_convert_fusion.6 = bf16[1024,512]{1,0:T(8,128)(2,1)S(1)} fusion(bf16[1024,512]{1,0:T(8,128)(2,1)} %add_convert_fusion.7, bf16[512,512]{1,0:T(8,128)(2,1)} %convolution_convert_fusion.5), kind=kOutput, calls=%fused_computation.29 | convolution fusion | flops 808714240 | bytes 2621440 | tf_op jit(solution)/shard_map/dot_general | solution.py:43
  201.6 21.5 %all-to-all-done.4 = bf16[16,64,512]{2,1,0:T(8,128)(2,1)} async-done(((bf16[16,64,512]{2,1,0:T(8,128)(2,1)}), bf16[16,64,512]{2,1,0:T(8,128)(2,1)}, u32[]{:S(2)}, u32[]{:S(2)}) %all-to-all-start.4) | async-done | bytes 1048608 | tf_op jit(solution)/shard_map/all_to_all | solution.py:21
  223.1 8.4 %all-to-all-start.2 = ((bf16[16,64,512]{2,1,0:T(8,128)(2,1)}), bf16[16,64,512]{2,1,0:T(8,128)(2,1)}, u32[]{:S(2)}, u32[]{:S(2)}) async-start(bf16[16,64,512]{2,1,0:T(8,128)(2,1)} %gather_fusion), calls=%async_computation.2 | async-start | bytes 2097152 | tf_op jit(solution)/shard_map/all_to_all | solution.py:21
  231.5 0.7 convolution_convert_fusion.4
  232.2 1.2 fusion.24
  233.7 1.6 fusion.25
  235.3 2.5 add_convert_fusion.4
  237.8 1.6 convolution_convert_fusion.3
  239.3 2.5 add_convert_fusion.3
  241.8 1.6 convolution_convert_fusion.2
  243.4 2.5 add_convert_fusion.2
  245.9 1.0 copy-done.11
  246.9 0.7 convolution_convert_fusion.1
  247.6 2.6 add_convert_fusion.1
  250.2 1.5 convolution_convert_fusion
  251.8 4.7 %fusion.7 = bf16[1024,512]{1,0:T(8,128)(2,1)} fusion(bf16[1024,512]{1,0:T(8,128)(2,1)} %bitcast.14, bf16[1024,512]{1,0:T(8,128)(2,1)} %copy-done.9, bf16[512,512]{1,0:T(8,128)(2,1)} %convolution_convert_fusion), kind=kOutput, calls=%fused_computation.18 | convolution fusion | flops 812908544 | bytes 3670016 | tf_op jit(solution)/shard_map/dot_general | solution.py:43
  256.5 24.8 %all-to-all-done.2 = bf16[16,64,512]{2,1,0:T(8,128)(2,1)} async-done(((bf16[16,64,512]{2,1,0:T(8,128)(2,1)}), bf16[16,64,512]{2,1,0:T(8,128)(2,1)}, u32[]{:S(2)}, u32[]{:S(2)}) %all-to-all-start.2) | async-done | bytes 1048608 | tf_op jit(solution)/shard_map/all_to_all | solution.py:21
  281.3 3.5 %convolution_bitcast_fusion.3 = f32[256,512]{0,1:T(8,128)} fusion(bf16[1024,512]{1,0:T(8,128)(2,1)} %bitcast.13, bf16[1024,512]{1,0:T(8,128)(2,1)S(1)} %copy-done.8, bf16[512,512]{1,0:T(8,128)(2,1)S(1)} %copy-done.6, bf16[1,1,256,1024]{3,2,1,0:T(8,128)(2,1)S(1)} %copy-done.4), kind=kOutput, calls=%fused_computation.77 | convolution fusion | flops 811597824 | bytes 3670016 | tf_op jit(solution)/shard_map/dot_general | solution.py:77
  284.8 1.8 fusion.33
  286.6 0.8 copy.11
  (27 shorter events, 0.3 us)
Async XLA Ops:
  0.6 114.7 %copy-start = (bf16[16,64,512]{2,1,0:T(8,128)(2,1)S(1)}, bf16[16,64,512]{2,1,0:T(8,128)(2,1)}, u32[]{:S(2)}) copy-start(bf16[16,64,512]{2,1,0:T(8,128)(2,1)} %param.7) | copy-start | bytes 3145732
  0.6 48.2 %copy-start.2 = (bf16[16,64,512]{2,1,0:T(8,128)(2,1)S(1)}, bf16[16,64,512]{2,1,0:T(8,128)(2,1)}, u32[]{:S(2)}) copy-start(bf16[16,64,512]{2,1,0:T(8,128)(2,1)} %param.6) | copy-start | bytes 3145732
  0.7 39.0 %copy-start.5 = (s32[1,16]{1,0:T(1,128)S(1)}, s32[1,16]{1,0:T(1,128)}, u32[]{:S(2)}) copy-start(s32[1,16]{1,0:T(1,128)} %param.8) | copy-start | bytes 196
  32.3 15.2 %all-to-all-start.1 = ((f32[32,8,128]{2,1,0:T(8,128)}), f32[32,8,128]{2,1,0:T(8,128)S(1)}, u32[]{:S(2)}, u32[]{:S(2)}) async-start(f32[32,8,128]{2,1,0:T(8,128)} %broadcast_in_dim.14), calls=%async_computation.1 | async-start | bytes 262144 | tf_op jit(solution)/shard_map/all_to_all | solution.py:27
  50.4 6.4 %copy-start.1 = (bf16[16,64,512]{2,1,0:T(8,128)(2,1)}, bf16[16,64,512]{2,1,0:T(8,128)(2,1)S(1)}, u32[]{:S(2)}) copy-start(bf16[16,64,512]{2,1,0:T(8,128)(2,1)S(1)} %fusion.2) | copy-start | bytes 3145732
  52.1 55.0 %all-to-all-start.3 = ((bf16[16,64,512]{2,1,0:T(8,128)(2,1)}), bf16[16,64,512]{2,1,0:T(8,128)(2,1)S(1)}, u32[]{:S(2)}, u32[]{:S(2)}) async-start(bf16[16,64,512]{2,1,0:T(8,128)(2,1)} %gather_fusion.1), calls=%async_computation.3 | async-start | bytes 2097152 | tf_op jit(solution)/shard_map/all_to_all | solution.py:21
  107.1 57.9 %all-to-all-start.5 = ((bf16[16,64,512]{2,1,0:T(8,128)(2,1)}), bf16[16,64,512]{2,1,0:T(8,128)(2,1)S(1)}, u32[]{:S(2)}, u32[]{:S(2)}) async-start(bf16[16,64,512]{2,1,0:T(8,128)(2,1)} %gather_fusion.3), calls=%async_computation.5 | async-start | bytes 2097152 | tf_op jit(solution)/shard_map/all_to_all | solution.py:21
  165.0 58.1 %all-to-all-start.4 = ((bf16[16,64,512]{2,1,0:T(8,128)(2,1)}), bf16[16,64,512]{2,1,0:T(8,128)(2,1)}, u32[]{:S(2)}, u32[]{:S(2)}) async-start(bf16[16,64,512]{2,1,0:T(8,128)(2,1)} %gather_fusion.2), calls=%async_computation.4 | async-start | bytes 2097152 | tf_op jit(solution)/shard_map/all_to_all | solution.py:21
  178.9 1.6 copy-start.3
  188.7 3.2 %copy-start.10 = (bf16[1024,512]{1,0:T(8,128)(2,1)S(1)}, bf16[1024,512]{1,0:T(8,128)(2,1)}, u32[]{:S(2)}) copy-start(bf16[1024,512]{1,0:T(8,128)(2,1)} %add_convert_fusion.8) | copy-start | bytes 3145732
  201.6 29.9 %copy-start.7 = (bf16[1024,512]{1,0:T(8,128)(2,1)}, bf16[1024,512]{1,0:T(8,128)(2,1)S(1)}, u32[]{:S(2)}) copy-start(bf16[1024,512]{1,0:T(8,128)(2,1)S(1)} %add_convert_fusion.6) | copy-start | bytes 3145732
  223.1 58.2 %all-to-all-start.2 = ((bf16[16,64,512]{2,1,0:T(8,128)(2,1)}), bf16[16,64,512]{2,1,0:T(8,128)(2,1)}, u32[]{:S(2)}, u32[]{:S(2)}) async-start(bf16[16,64,512]{2,1,0:T(8,128)(2,1)} %gather_fusion), calls=%async_computation.2 | async-start | bytes 2097152 | tf_op jit(solution)/shard_map/all_to_all | solution.py:21
  245.9 1.0 copy-start.11
  250.2 1.6 copy-start.9
  251.8 29.5 %copy-start.4 = (bf16[1,1,256,1024]{3,2,1,0:T(8,128)(2,1)S(1)}, bf16[1,1,256,1024]{3,2,1,0:T(8,128)(2,1)}, u32[]{:S(2)}) copy-start(bf16[1,1,256,1024]{3,2,1,0:T(8,128)(2,1)} %param.9) | copy-start | bytes 1572868
  251.8 29.5 %copy-start.6 = (bf16[512,512]{1,0:T(8,128)(2,1)S(1)}, bf16[512,512]{1,0:T(8,128)(2,1)}, u32[]{:S(2)}) copy-start(bf16[512,512]{1,0:T(8,128)(2,1)} %fusion.24) | copy-start | bytes 1572868
  251.8 29.5 %copy-start.8 = (bf16[1024,512]{1,0:T(8,128)(2,1)S(1)}, bf16[1024,512]{1,0:T(8,128)(2,1)}, u32[]{:S(2)}) copy-start(bf16[1024,512]{1,0:T(8,128)(2,1)} %copy-done.7) | copy-start | bytes 3145732

commit v2 on v1

v2 whole, which is shorter than its diff:
```python
import functools
import math

import jax
import jax.numpy as jnp
from jax import lax
from jax.experimental import pallas as pl
from jax.experimental.pallas import tpu as pltpu
from jax.sharding import Mesh
from jax.sharding import PartitionSpec as P


D = 1024
F = 512
ITERS = 5
GROUP = ("group_0", "group_1", "group_2")

coefficients = (3.4445, -4.775, 2.0315)
momentum_decay = 0.95
learning_rate = 0.05
clip_rms = 0.5

FAR = (8, 7, 9, 6, 10)
NEAR = (5, 11, 4, 12, 3, 13, 2, 14, 1, 15)
LATE = (3, 13, 2, 14, 1, 15)


def total_over(value, axes):
    peers = math.prod(lax.axis_size(axis) for axis in axes)
    mine = jnp.broadcast_to(value, (peers, 8, 128))
    theirs = lax.all_to_all(mine, axes, split_axis=0, concat_axis=0, tiled=True)
    return jnp.sum(theirs[:, 0, 0])


def orthogonal_kernel(state_ref, update_ref, iterate_ref):
    rows = iterate_ref.shape[0]
    widened = state_ref[...].reshape(rows, F).astype(jnp.float32)
    inverse_norm = 1.0 / (jnp.sqrt(jnp.sum(widened * widened)) + 1e-07)
    iterate_ref[...] = (widened * inverse_norm).astype(jnp.bfloat16)

    def iteration(_, carry):
        iterate = iterate_ref[...]
        gram = lax.dot_general(
            iterate, iterate, (((0,), (0,)), ((), ())), preferred_element_type=jnp.float32
        ).astype(jnp.bfloat16)
        squared = jnp.dot(gram, gram, preferred_element_type=jnp.float32)
        polynomial = (
            coefficients[1] * gram.astype(jnp.float32) + coefficients[2] * squared
        ).astype(jnp.bfloat16)
        product = jnp.dot(iterate, polynomial, preferred_element_type=jnp.float32)
        iterate_ref[...] = (coefficients[0] * iterate.astype(jnp.float32) + product).astype(
            jnp.bfloat16
        )
        return carry

    lax.fori_loop(0, ITERS, iteration, 0)
    update_ref[...] = (
        (0.2 * math.sqrt(D) * iterate_ref[...].astype(jnp.float32))
        .astype(jnp.bfloat16)
        .reshape(update_ref.shape)
    )


def orthogonal(states):
    shards, matrices, rows, _ = states.shape
    return pl.pallas_call(
        orthogonal_kernel,
        grid=(matrices,),
        in_specs=[pl.BlockSpec((shards, 1, rows, F), lambda k: (0, k, 0, 0))],
        out_specs=pl.BlockSpec((1, shards * rows, F), lambda k: (k, 0, 0)),
        out_shape=jax.ShapeDtypeStruct((matrices, shards * rows, F), jnp.bfloat16),
        scratch_shapes=[pltpu.VMEM((shards * rows, F), jnp.bfloat16)],
        cost_estimate=pl.CostEstimate(flops=13_000_000_000, transcendentals=0, bytes_accessed=4 << 20),
    )(states)


def pick_kernel(slots_ref, position_ref, weights_ref, *out_refs):
    shards = len(out_refs)
    for distance, out_ref in enumerate(out_refs):
        slot = lax.rem(position_ref[0] + distance, shards)
        out_ref[...] = weights_ref[slots_ref[slot]]


def picked_by_distance(slots, position, paired):
    shards = slots.shape[0]
    smem = pl.BlockSpec(memory_space=pltpu.SMEM)
    vmem = pl.BlockSpec(memory_space=pltpu.VMEM)
    return pl.pallas_call(
        pick_kernel,
        in_specs=[smem, smem, vmem],
        out_specs=[vmem] * shards,
        out_shape=[jax.ShapeDtypeStruct(paired.shape[1:], paired.dtype)] * shards,
    )(slots, position, paired)


def add_blocks(position, distances, blocks, prompt_ref, update_ref, outs):
    shards, _, rows = prompt_ref.shape
    for distance, block in zip(distances, blocks, strict=True):
        source = lax.rem(position + (shards - distance), shards)
        at = pl.multiple_of(source * rows, rows)
        part = prompt_ref[source]
        for k in range(2):
            old = block[k].astype(jnp.float32)
            update = update_ref[k, pl.ds(at, rows), :].astype(jnp.float32)
            new = (old - learning_rate * update).astype(jnp.bfloat16)
            product = jnp.dot(part, new, preferred_element_type=jnp.float32)
            outs[k] = product if outs[k] is None else outs[k] + product


def early_kernel(distances, position_ref, prompt_ref, update_ref, *refs):
    *blocks, out_ref = refs
    outs = [None, None]
    add_blocks(position_ref[0], distances, blocks, prompt_ref, update_ref, outs)
    out_ref[0] = outs[0]
    out_ref[1] = outs[1]


def late_kernel(distances, position_ref, prompt_ref, update_ref, sums_ref, *refs):
    *blocks, out_ref = refs
    outs = [sums_ref[0], sums_ref[1]]
    add_blocks(position_ref[0], distances, blocks, prompt_ref, update_ref, outs)
    gate, up = outs
    out_ref[...] = (gate / (1.0 + jnp.exp(-gate)) * up).astype(jnp.bfloat16)


def step_and_prefill(momentum, gradient, weights, slot_map, tokens):
    shards = lax.axis_size("shard")
    every_entry = shards * lax.axis_size(GROUP) * D * F
    rows = weights.shape[1]
    position = lax.axis_index("shard")
    slots = slot_map[0]
    paired = weights.reshape(shards // 2, 2, rows, F)

    at = position.reshape(1).astype(jnp.int32)
    mine = picked_by_distance(slots, at, paired)
    old = {0: mine[0]}
    for distance in (*FAR, *NEAR):
        old[distance] = lax.ppermute(
            mine[distance], "shard", [(k, (k + distance) % shards) for k in range(shards)]
        )

    widened = gradient.astype(jnp.float32)
    grand_total = jnp.sum(widened * widened)
    grand_total = total_over(grand_total, ("shard",))
    grand_total = total_over(grand_total, GROUP)
    clip_factor = jnp.minimum(
        1.0, clip_rms * math.sqrt(every_entry) / jnp.sqrt(grand_total + 1e-06)
    )
    fresh_state = (momentum_decay * momentum.astype(jnp.float32) + clip_factor * widened).astype(
        jnp.bfloat16
    )
    picked = fresh_state.reshape(paired.shape).at[slots].get(mode="promise_in_bounds")
    states = lax.all_to_all(picked, "shard", split_axis=0, concat_axis=0, tiled=True)
    update = orthogonal(states)

    prompt = jnp.moveaxis(tokens[0, 0].reshape(-1, shards, rows), 1, 0)
    early = tuple(d for d in old if d not in LATE)
    smem = pl.BlockSpec(memory_space=pltpu.SMEM)
    vmem = pl.BlockSpec(memory_space=pltpu.VMEM)
    count = prompt.shape[1]
    sums = pl.pallas_call(
        functools.partial(early_kernel, early),
        in_specs=[smem] + [vmem] * (2 + len(early)),
        out_specs=vmem,
        out_shape=jax.ShapeDtypeStruct((2, count, F), jnp.float32),
    )(at, prompt, update, *(old[d] for d in early))
    hidden = pl.pallas_call(
        functools.partial(late_kernel, LATE),
        in_specs=[smem] + [vmem] * (3 + len(LATE)),
        out_specs=vmem,
        out_shape=jax.ShapeDtypeStruct((count, F), jnp.bfloat16),
    )(at, prompt, update, sums, *(old[d] for d in LATE))
    return (fresh_state, hidden[None, None])


def solution(mesh):
    split = Mesh(
        mesh.devices.reshape(mesh.shape["shard"], 4, 4, 2),
        ("shard", "group_0", "group_1", "group_2"),
    )
    placed = (
        P(GROUP, "shard", None),
        P(GROUP, "shard", None),
        P(GROUP, "shard", None),
        P(GROUP, None),
        P("shard", GROUP, None, None),
    )
    return jax.shard_map(
        step_and_prefill,
        mesh=split,
        in_specs=placed,
        out_specs=(P(GROUP, "shard", None), P("shard", GROUP, None, None)),
        check_vma=False,
    )
```

time: 288 us -> 273 us (0.948)
  starting transfers between devices: 37 us -> 101 us
  waiting for transfers between devices: 151 us -> 95.9 us
  matrix products: 51.7 us -> 0 us
  Pallas kernels: 0 us -> 33 us
    all_to_all x4 -> x1, waiting for transfers between devices: 143 us -> 0.01 us  [step_and_prefill(): lax.all_to_all(picked, 'shard', split_axis=0, concat_axis=0, tiled=True)]
    ppermute x0 -> x15, waiting for transfers between devices: none -> 88.7 us  [step_and_prefill(): lax.ppermute(mine[distance], 'shard', [(k, (k + distance) % shards) for k...]
    ppermute x0 -> x15, starting transfers between devices: none -> 88.4 us  [step_and_prefill(): lax.ppermute(mine[distance], 'shard', [(k, (k + distance) % shards) for k...]
    dot_general x22 -> x0, matrix products: 51.7 us -> none  [the longest x9 28.1 us: orthogonal(): product = jnp.dot(iterate, polynomial, preferred_element_type=jnp.float32)]
    pallas_call x0 -> x4, Pallas kernels: none -> 33 us  [the longest x1 21.5 us: orthogonal(): pl.pallas_call(orthogonal_kernel, grid=(matrices,), in_specs=[pl.BlockSpe...]
    all_to_all x4 -> x1, starting transfers between devices: 29.7 us -> 4.93 us  [step_and_prefill(): lax.all_to_all(picked, 'shard', split_axis=0, concat_axis=0, tiled=True)]
    gather x4 -> x1, local copies, waits for them, and re-layouts: 6.4 us -> 2.01 us  [step_and_prefill(): fresh_state.reshape(paired.shape).at[slots].get(mode='promise_in_bounds')]
  transfers between devices with their start and end apart: 5 -> 17, of which waited for: 5 -> 4; matrix products, arithmetic and copies ran while one was open for 19% -> 1% of each run, Pallas kernels for 0% -> 11%
where the time goes in v2:
time: 273 us
  starting transfers between devices  101 us (37%)
  waiting for transfers between devices  95.9 us (35%)
  Pallas kernels  33 us (12%)
  blocking collectives  26.5 us (10%)
  local copies, waits for them, and re-layouts  8.86 us (3%)
  other arithmetic  5.98 us (2%)
    ppermute x15, waiting for transfers between devices, step_and_prefill(): lax.ppermute(mine[distance], 'shard', [(k, (k + distance) % shards) for k...  88.7 us
    ppermute x15, starting transfers between devices, step_and_prefill(): lax.ppermute(mine[distance], 'shard', [(k, (k + distance) % shards) for k...  88.4 us
    all_to_all x1, blocking collectives, total_over(): theirs = lax.all_to_all(mine, axes, split_axis=0, concat_axis=0, tiled=True)  26.5 us
    pallas_call x1, Pallas kernels, orthogonal(): pl.pallas_call(orthogonal_kernel, grid=(matrices,), in_specs=[pl.BlockSpe...  21.5 us
    all_to_all x1, starting transfers between devices, total_over(): theirs = lax.all_to_all(mine, axes, split_axis=0, concat_axis=0, tiled=True)  7.32 us
    all_to_all x1, waiting for transfers between devices, total_over(): theirs = lax.all_to_all(mine, axes, split_axis=0, concat_axis=0, tiled=True)  7.16 us
  transfers between devices with their start and end apart: 17, of which 4 were waited for; matrix products, arithmetic and copies ran while one was open for 1% of the time, Pallas kernels for 11%

profile of v2, /device:TPU:32, one launch (start us, length us, event | category | flops | bytes accessed | tf_op | source)
XLA Modules:
  0.0 272.5 jit_solution(3738463161123907233)
XLA Ops:
  0.6 2.5 fusion
  3.1 0.6 broadcast_in_dim.10
  3.8 26.5 %all_to_all.15 = f32[16,8,128]{2,1,0:T(8,128)S(1)} all-to-all(f32[16,8,128]{2,1,0:T(8,128)S(1)} %broadcast_in_dim.10), channel_id=1, replica_groups=mesh['shard'=16,'group_0'=4,'group_1'=4,'group_2'=2] {'shard'}, dimensions={0} | all-to-all | bytes 131072 | tf_op jit(solution)/shard_map/all_to_all | solution.py:31
  30.3 0.6 slice_reduce_fusion.1
  30.9 1.3 broadcast_in_dim.11
  32.2 7.3 %all-to-all-start.1 = ((f32[32,8,128]{2,1,0:T(8,128)}), f32[32,8,128]{2,1,0:T(8,128)S(1)}, u32[]{:S(2)}, u32[]{:S(2)}) async-start(f32[32,8,128]{2,1,0:T(8,128)} %broadcast_in_dim.11), calls=%async_computation.1 | async-start | bytes 262144 | tf_op jit(solution)/shard_map/all_to_all | solution.py:31
  39.5 0.7 fusion.3
  40.2 7.2 %all-to-all-done.1 = f32[32,8,128]{2,1,0:T(8,128)S(1)} async-done(((f32[32,8,128]{2,1,0:T(8,128)}), f32[32,8,128]{2,1,0:T(8,128)S(1)}, u32[]{:S(2)}, u32[]{:S(2)}) %all-to-all-start.1) | async-done | bytes 131104 | tf_op jit(solution)/shard_map/all_to_all | solution.py:31
  47.4 0.6 slice_reduce_fusion
  48.7 1.6 fusion.2
  50.3 0.0 copy-start
  50.3 2.0 gather_fusion
  52.4 4.9 %all-to-all-start.2 = ((bf16[16,2,64,512]{3,2,1,0:T(8,128)(2,1)}), bf16[16,2,64,512]{3,2,1,0:T(8,128)(2,1)S(1)}, u32[]{:S(2)}, u32[]{:S(2)}) async-start(bf16[16,2,64,512]{3,2,1,0:T(8,128)(2,1)} %gather_fusion), calls=%async_computation.2 | async-start | bytes 4194304 | tf_op jit(solution)/shard_map/all_to_all | solution.py:153
  57.3 2.7 shard_map.69
  60.0 11.2 %collective-permute-start = (bf16[2,64,512]{2,1,0:T(8,128)(2,1)}, bf16[2,64,512]{2,1,0:T(8,128)(2,1)S(1)}, u32[]{:S(2)}, u32[]{:S(2)}) collective-permute-start(bf16[2,64,512]{2,1,0:T(8,128)(2,1)} %get-tuple-element.19), channel_id=1, source_target_pairs={{0,256},{32,288},{64,320},{96,352},{128,384},{160,416},{192,448},{... | collective-permute-start | bytes 393224 | tf_op jit(solution)/shard_map/ppermute | solution.py:138
  71.2 2.1 collective-permute-start.1
  73.3 11.6 %collective-permute-start.2 = (bf16[2,64,512]{2,1,0:T(8,128)(2,1)}, bf16[2,64,512]{2,1,0:T(8,128)(2,1)S(1)}, u32[]{:S(2)}, u32[]{:S(2)}) collective-permute-start(bf16[2,64,512]{2,1,0:T(8,128)(2,1)} %get-tuple-element.21), channel_id=1, source_target_pairs={{0,288},{32,320},{64,352},{96,384},{128,416},{160,448},{192,480},{... | collective-permute-start | bytes 393224 | tf_op jit(solution)/shard_map/ppermute | solution.py:138
  84.9 1.9 collective-permute-start.3
  86.8 10.8 %collective-permute-start.4 = (bf16[2,64,512]{2,1,0:T(8,128)(2,1)}, bf16[2,64,512]{2,1,0:T(8,128)(2,1)S(1)}, u32[]{:S(2)}, u32[]{:S(2)}) collective-permute-start(bf16[2,64,512]{2,1,0:T(8,128)(2,1)} %get-tuple-element.23), channel_id=1, source_target_pairs={{0,320},{32,352},{64,384},{96,416},{128,448},{160,480},{192,0},{22... | collective-permute-start | bytes 393224 | tf_op jit(solution)/shard_map/ppermute | solution.py:138
  97.6 70.8 %collective-permute-done.refs_1_ = bf16[2,64,512]{2,1,0:T(8,128)(2,1)S(1)} collective-permute-done((bf16[2,64,512]{2,1,0:T(8,128)(2,1)}, bf16[2,64,512]{2,1,0:T(8,128)(2,1)S(1)}, u32[]{:S(2)}, u32[]{:S(2)}) %collective-permute-start) | collective-permute-done | bytes 131104 | tf_op jit(solution)/shard_map/ppermute | solution.py:138
  168.4 6.9 %collective-permute-start.5 = (bf16[2,64,512]{2,1,0:T(8,128)(2,1)}, bf16[2,64,512]{2,1,0:T(8,128)(2,1)}, u32[]{:S(2)}, u32[]{:S(2)}) collective-permute-start(bf16[2,64,512]{2,1,0:T(8,128)(2,1)} %get-tuple-element.24), channel_id=1, source_target_pairs={{0,160},{32,192},{64,224},{96,256},{128,288},{160,320},{192,352},{... | collective-permute-start | bytes 393224 | tf_op jit(solution)/shard_map/ppermute | solution.py:138
  175.4 10.7 %collective-permute-done.1.refs_2_ = bf16[2,64,512]{2,1,0:T(8,128)(2,1)S(1)} collective-permute-done((bf16[2,64,512]{2,1,0:T(8,128)(2,1)}, bf16[2,64,512]{2,1,0:T(8,128)(2,1)S(1)}, u32[]{:S(2)}, u32[]{:S(2)}) %collective-permute-start.1) | collective-permute-done | bytes 131104 | tf_op jit(solution)/shard_map/ppermute | solution.py:138
  186.0 9.2 %collective-permute-start.6 = (bf16[2,64,512]{2,1,0:T(8,128)(2,1)}, bf16[2,64,512]{2,1,0:T(8,128)(2,1)}, u32[]{:S(2)}, u32[]{:S(2)}) collective-permute-start(bf16[2,64,512]{2,1,0:T(8,128)(2,1)} %get-tuple-element.25), channel_id=1, source_target_pairs={{0,352},{32,384},{64,416},{96,448},{128,480},{160,0},{192,32},{224... | collective-permute-start | bytes 393224 | tf_op jit(solution)/shard_map/ppermute | solution.py:138
  195.3 2.3 collective-permute-start.7
  197.6 7.2 %collective-permute-done.3.refs_4_ = bf16[2,64,512]{2,1,0:T(8,128)(2,1)S(1)} collective-permute-done((bf16[2,64,512]{2,1,0:T(8,128)(2,1)}, bf16[2,64,512]{2,1,0:T(8,128)(2,1)S(1)}, u32[]{:S(2)}, u32[]{:S(2)}) %collective-permute-start.3) | collective-permute-done | bytes 131104 | tf_op jit(solution)/shard_map/ppermute | solution.py:138
  204.8 2.0 collective-permute-start.8
  206.8 0.0 collective-permute-done.4.refs_5_
  206.9 0.6 copy-done.8
  207.5 11.7 %collective-permute-start.9 = (bf16[2,64,512]{2,1,0:T(8,128)(2,1)}, bf16[2,64,512]{2,1,0:T(8,128)(2,1)}, u32[]{:S(2)}, u32[]{:S(2)}) collective-permute-start(bf16[2,64,512]{2,1,0:T(8,128)(2,1)} %get-tuple-element.28), channel_id=1, source_target_pairs={{0,96},{32,128},{64,160},{96,192},{128,224},{160,256},{192,288},{2... | collective-permute-start | bytes 393224 | tf_op jit(solution)/shard_map/ppermute | solution.py:138
  219.2 0.2 copy.13
  219.4 1.4 copy.14
  220.8 0.0 collective-permute-done.5.refs_6_
  220.8 1.9 collective-permute-start.10
  222.7 0.0 collective-permute-done.6.refs_7_
  222.7 6.1 %collective-permute-start.11 = (bf16[2,64,512]{2,1,0:T(8,128)(2,1)}, bf16[2,64,512]{2,1,0:T(8,128)(2,1)S(1)}, u32[]{:S(2)}, u32[]{:S(2)}) collective-permute-start(bf16[2,64,512]{2,1,0:T(8,128)(2,1)} %get-tuple-element.30), channel_id=1, source_target_pairs={{0,64},{32,96},{64,128},{96,160},{128,192},{160,224},{192,256},{22... | collective-permute-start | bytes 393224 | tf_op jit(solution)/shard_map/ppermute | solution.py:138
  228.8 3.0 %collective-permute-start.12 = (bf16[2,64,512]{2,1,0:T(8,128)(2,1)}, bf16[2,64,512]{2,1,0:T(8,128)(2,1)S(1)}, u32[]{:S(2)}, u32[]{:S(2)}) collective-permute-start(bf16[2,64,512]{2,1,0:T(8,128)(2,1)} %get-tuple-element.31), channel_id=1, source_target_pairs={{0,448},{32,480},{64,0},{96,32},{128,64},{160,96},{192,128},{224,1... | collective-permute-start | bytes 393224 | tf_op jit(solution)/shard_map/ppermute | solution.py:138
  231.8 0.0 collective-permute-done.8.refs_9_
  231.9 4.3 %collective-permute-start.13 = (bf16[2,64,512]{2,1,0:T(8,128)(2,1)}, bf16[2,64,512]{2,1,0:T(8,128)(2,1)S(1)}, u32[]{:S(2)}, u32[]{:S(2)}) collective-permute-start(bf16[2,64,512]{2,1,0:T(8,128)(2,1)} %get-tuple-element.32), channel_id=1, source_target_pairs={{0,32},{32,64},{64,96},{96,128},{128,160},{160,192},{192,224},{224... | collective-permute-start | bytes 393224 | tf_op jit(solution)/shard_map/ppermute | solution.py:138
  236.2 3.2 %collective-permute-start.14 = (bf16[2,64,512]{2,1,0:T(8,128)(2,1)}, bf16[2,64,512]{2,1,0:T(8,128)(2,1)S(1)}, u32[]{:S(2)}, u32[]{:S(2)}) collective-permute-start(bf16[2,64,512]{2,1,0:T(8,128)(2,1)} %get-tuple-element.33), channel_id=1, source_target_pairs={{0,480},{32,0},{64,32},{96,64},{128,96},{160,128},{192,160},{224,1... | collective-permute-start | bytes 393224 | tf_op jit(solution)/shard_map/ppermute | solution.py:138
  239.4 1.3 copy-done.2
  240.7 21.5 %shard_map.68.update_ref = bf16[2,1024,512]{2,1,0:T(8,128)(2,1)} custom-call(bf16[16,2,64,512]{3,2,1,0:T(8,128)(2,1)} %copy-done.2), custom_call_target="tpu_custom_call" | custom-call | flops 12999999488 | bytes 4194304 | tf_op jit(solution)/shard_map/pallas_call | solution.py:66
  262.3 4.7 %shard_map.70.sums_ref = f32[2,256,512]{2,1,0:T(8,128)} custom-call(s32[1]{0:T(128)} %bitcast.position_ref, bf16[16,256,64]{2,1,0:T(8,128)(2,1)} %bitcast.12, bf16[2,1024,512]{2,1,0:T(8,128)(2,1)} %shard_map.68.update_ref, bf16[2,64,512]{2,1,0:T(8,128)(2,1)} %get-tuple-element.18.refs_0_, bf16[2,64,512]{2,1,0:T(8,128)(2,1)} %copy-done.4, ...), custom_call_target="tpu_custom_call" | custom-call | tf_op jit(solution)/shard_map/pallas_call | solution.py:161
  267.1 0.6 copy-done.9
  267.6 0.1 copy-done.10
  267.7 0.0 copy-done.11
  267.7 0.1 copy-done.12
  267.8 0.7 copy-done.13
  268.5 4.1 %shard_map.71 = bf16[256,512]{1,0:T(8,128)(2,1)} custom-call(s32[1]{0:T(128)} %bitcast.position_ref, bf16[16,256,64]{2,1,0:T(8,128)(2,1)} %bitcast.13, bf16[2,1024,512]{2,1,0:T(8,128)(2,1)} %shard_map.68.update_ref, f32[2,256,512]{2,1,0:T(8,128)} %shard_map.70.sums_ref, bf16[2,64,512]{2,1,0:T(8,128)(2,1)} %collective-permute-done.9.refs_0_, ...), custom_call_target="tpu_custom_call" | custom-call | tf_op jit(solution)/shard_map/pallas_call | solution.py:167
  (30 shorter events, 0.1 us)
Async XLA Ops:
  0.6 48.1 %copy-start.1 = (bf16[16,64,512]{2,1,0:T(8,128)(2,1)S(1)}, bf16[16,64,512]{2,1,0:T(8,128)(2,1)}, u32[]{:S(2)}) copy-start(bf16[16,64,512]{2,1,0:T(8,128)(2,1)} %param.6) | copy-start | bytes 3145732
  32.2 15.2 %all-to-all-start.1 = ((f32[32,8,128]{2,1,0:T(8,128)}), f32[32,8,128]{2,1,0:T(8,128)S(1)}, u32[]{:S(2)}, u32[]{:S(2)}) async-start(f32[32,8,128]{2,1,0:T(8,128)} %broadcast_in_dim.11), calls=%async_computation.1 | async-start | bytes 262144 | tf_op jit(solution)/shard_map/all_to_all | solution.py:31
  50.3 2.0 copy-start
  52.3 166.8 %copy-start.3 = (bf16[1,1,256,1024]{3,2,1,0:T(8,128)(2,1)S(1)}, bf16[1,1,256,1024]{3,2,1,0:T(8,128)(2,1)}, u32[]{:S(2)}) copy-start(bf16[1,1,256,1024]{3,2,1,0:T(8,128)(2,1)} %param.9) | copy-start | bytes 1572868
  52.4 187.1 %all-to-all-start.2 = ((bf16[16,2,64,512]{3,2,1,0:T(8,128)(2,1)}), bf16[16,2,64,512]{3,2,1,0:T(8,128)(2,1)S(1)}, u32[]{:S(2)}, u32[]{:S(2)}) async-start(bf16[16,2,64,512]{3,2,1,0:T(8,128)(2,1)} %gather_fusion), calls=%async_computation.2 | async-start | bytes 4194304 | tf_op jit(solution)/shard_map/all_to_all | solution.py:153
  60.0 108.5 %collective-permute-start = (bf16[2,64,512]{2,1,0:T(8,128)(2,1)}, bf16[2,64,512]{2,1,0:T(8,128)(2,1)S(1)}, u32[]{:S(2)}, u32[]{:S(2)}) collective-permute-start(bf16[2,64,512]{2,1,0:T(8,128)(2,1)} %get-tuple-element.19), channel_id=1, source_target_pairs={{0,256},{32,288},{64,320},{96,352},{128,384},{160,416},{192,448},{... | collective-permute-start | bytes 393224 | tf_op jit(solution)/shard_map/ppermute | solution.py:138
  71.2 114.8 %collective-permute-start.1 = (bf16[2,64,512]{2,1,0:T(8,128)(2,1)}, bf16[2,64,512]{2,1,0:T(8,128)(2,1)S(1)}, u32[]{:S(2)}, u32[]{:S(2)}) collective-permute-start(bf16[2,64,512]{2,1,0:T(8,128)(2,1)} %get-tuple-element.20), channel_id=1, source_target_pairs={{0,224},{32,256},{64,288},{96,320},{128,352},{160,384},{192,416},{... | collective-permute-start | bytes 393224 | tf_op jit(solution)/shard_map/ppermute | solution.py:138
  73.3 122.0 %collective-permute-start.2 = (bf16[2,64,512]{2,1,0:T(8,128)(2,1)}, bf16[2,64,512]{2,1,0:T(8,128)(2,1)S(1)}, u32[]{:S(2)}, u32[]{:S(2)}) collective-permute-start(bf16[2,64,512]{2,1,0:T(8,128)(2,1)} %get-tuple-element.21), channel_id=1, source_target_pairs={{0,288},{32,320},{64,352},{96,384},{128,416},{160,448},{192,480},{... | collective-permute-start | bytes 393224 | tf_op jit(solution)/shard_map/ppermute | solution.py:138
  84.9 119.9 %collective-permute-start.3 = (bf16[2,64,512]{2,1,0:T(8,128)(2,1)}, bf16[2,64,512]{2,1,0:T(8,128)(2,1)S(1)}, u32[]{:S(2)}, u32[]{:S(2)}) collective-permute-start(bf16[2,64,512]{2,1,0:T(8,128)(2,1)} %get-tuple-element.22), channel_id=1, source_target_pairs={{0,192},{32,224},{64,256},{96,288},{128,320},{160,352},{192,384},{... | collective-permute-start | bytes 393224 | tf_op jit(solution)/shard_map/ppermute | solution.py:138
  86.8 120.0 %collective-permute-start.4 = (bf16[2,64,512]{2,1,0:T(8,128)(2,1)}, bf16[2,64,512]{2,1,0:T(8,128)(2,1)S(1)}, u32[]{:S(2)}, u32[]{:S(2)}) collective-permute-start(bf16[2,64,512]{2,1,0:T(8,128)(2,1)} %get-tuple-element.23), channel_id=1, source_target_pairs={{0,320},{32,352},{64,384},{96,416},{128,448},{160,480},{192,0},{22... | collective-permute-start | bytes 393224 | tf_op jit(solution)/shard_map/ppermute | solution.py:138
  168.4 93.9 %copy-start.4 = (bf16[2,64,512]{2,1,0:T(8,128)(2,1)}, bf16[2,64,512]{2,1,0:T(8,128)(2,1)S(1)}, u32[]{:S(2)}) copy-start(bf16[2,64,512]{2,1,0:T(8,128)(2,1)S(1)} %collective-permute-done.refs_1_) | copy-start | bytes 393220
  168.4 52.3 %collective-permute-start.5 = (bf16[2,64,512]{2,1,0:T(8,128)(2,1)}, bf16[2,64,512]{2,1,0:T(8,128)(2,1)}, u32[]{:S(2)}, u32[]{:S(2)}) collective-permute-start(bf16[2,64,512]{2,1,0:T(8,128)(2,1)} %get-tuple-element.24), channel_id=1, source_target_pairs={{0,160},{32,192},{64,224},{96,256},{128,288},{160,320},{192,352},{... | collective-permute-start | bytes 393224 | tf_op jit(solution)/shard_map/ppermute | solution.py:138
  186.0 76.2 %copy-start.5 = (bf16[2,64,512]{2,1,0:T(8,128)(2,1)}, bf16[2,64,512]{2,1,0:T(8,128)(2,1)S(1)}, u32[]{:S(2)}) copy-start(bf16[2,64,512]{2,1,0:T(8,128)(2,1)S(1)} %collective-permute-done.1.refs_2_) | copy-start | bytes 393220
  186.0 36.6 %collective-permute-start.6 = (bf16[2,64,512]{2,1,0:T(8,128)(2,1)}, bf16[2,64,512]{2,1,0:T(8,128)(2,1)}, u32[]{:S(2)}, u32[]{:S(2)}) collective-permute-start(bf16[2,64,512]{2,1,0:T(8,128)(2,1)} %get-tuple-element.25), channel_id=1, source_target_pairs={{0,352},{32,384},{64,416},{96,448},{128,480},{160,0},{192,32},{224... | collective-permute-start | bytes 393224 | tf_op jit(solution)/shard_map/ppermute | solution.py:138
  195.3 67.0 %copy-start.6 = (bf16[2,64,512]{2,1,0:T(8,128)(2,1)}, bf16[2,64,512]{2,1,0:T(8,128)(2,1)S(1)}, u32[]{:S(2)}) copy-start(bf16[2,64,512]{2,1,0:T(8,128)(2,1)S(1)} %collective-permute-done.2.refs_3_) | copy-start | bytes 393220
  195.3 33.5 %collective-permute-start.7 = (bf16[2,64,512]{2,1,0:T(8,128)(2,1)}, bf16[2,64,512]{2,1,0:T(8,128)(2,1)}, u32[]{:S(2)}, u32[]{:S(2)}) collective-permute-start(bf16[2,64,512]{2,1,0:T(8,128)(2,1)} %get-tuple-element.26), channel_id=1, source_target_pairs={{0,128},{32,160},{64,192},{96,224},{128,256},{160,288},{192,320},{... | collective-permute-start | bytes 393224 | tf_op jit(solution)/shard_map/ppermute | solution.py:138
  204.8 2.0 copy-start.7
  204.8 27.0 %collective-permute-start.8 = (bf16[2,64,512]{2,1,0:T(8,128)(2,1)}, bf16[2,64,512]{2,1,0:T(8,128)(2,1)}, u32[]{:S(2)}, u32[]{:S(2)}) collective-permute-start(bf16[2,64,512]{2,1,0:T(8,128)(2,1)} %get-tuple-element.27), channel_id=1, source_target_pairs={{0,384},{32,416},{64,448},{96,480},{128,0},{160,32},{192,64},{224,... | collective-permute-start | bytes 393224 | tf_op jit(solution)/shard_map/ppermute | solution.py:138
  206.8 0.6 copy-start.8
  207.5 28.7 %collective-permute-start.9 = (bf16[2,64,512]{2,1,0:T(8,128)(2,1)}, bf16[2,64,512]{2,1,0:T(8,128)(2,1)}, u32[]{:S(2)}, u32[]{:S(2)}) collective-permute-start(bf16[2,64,512]{2,1,0:T(8,128)(2,1)} %get-tuple-element.28), channel_id=1, source_target_pairs={{0,96},{32,128},{64,160},{96,192},{128,224},{160,256},{192,288},{2... | collective-permute-start | bytes 393224 | tf_op jit(solution)/shard_map/ppermute | solution.py:138
  220.8 46.2 %collective-permute-start.10 = (bf16[2,64,512]{2,1,0:T(8,128)(2,1)}, bf16[2,64,512]{2,1,0:T(8,128)(2,1)S(1)}, u32[]{:S(2)}, u32[]{:S(2)}) collective-permute-start(bf16[2,64,512]{2,1,0:T(8,128)(2,1)} %get-tuple-element.29), channel_id=1, source_target_pairs={{0,416},{32,448},{64,480},{96,0},{128,32},{160,64},{192,96},{224,1... | collective-permute-start | bytes 393224 | tf_op jit(solution)/shard_map/ppermute | solution.py:138
  222.7 44.3 %collective-permute-start.11 = (bf16[2,64,512]{2,1,0:T(8,128)(2,1)}, bf16[2,64,512]{2,1,0:T(8,128)(2,1)S(1)}, u32[]{:S(2)}, u32[]{:S(2)}) collective-permute-start(bf16[2,64,512]{2,1,0:T(8,128)(2,1)} %get-tuple-element.30), channel_id=1, source_target_pairs={{0,64},{32,96},{64,128},{96,160},{128,192},{160,224},{192,256},{22... | collective-permute-start | bytes 393224 | tf_op jit(solution)/shard_map/ppermute | solution.py:138
  228.8 38.2 %collective-permute-start.12 = (bf16[2,64,512]{2,1,0:T(8,128)(2,1)}, bf16[2,64,512]{2,1,0:T(8,128)(2,1)S(1)}, u32[]{:S(2)}, u32[]{:S(2)}) collective-permute-start(bf16[2,64,512]{2,1,0:T(8,128)(2,1)} %get-tuple-element.31), channel_id=1, source_target_pairs={{0,448},{32,480},{64,0},{96,32},{128,64},{160,96},{192,128},{224,1... | collective-permute-start | bytes 393224 | tf_op jit(solution)/shard_map/ppermute | solution.py:138
  231.9 35.2 %collective-permute-start.13 = (bf16[2,64,512]{2,1,0:T(8,128)(2,1)}, bf16[2,64,512]{2,1,0:T(8,128)(2,1)S(1)}, u32[]{:S(2)}, u32[]{:S(2)}) collective-permute-start(bf16[2,64,512]{2,1,0:T(8,128)(2,1)} %get-tuple-element.32), channel_id=1, source_target_pairs={{0,32},{32,64},{64,96},{96,128},{128,160},{160,192},{192,224},{224... | collective-permute-start | bytes 393224 | tf_op jit(solution)/shard_map/ppermute | solution.py:138
  236.2 30.9 %collective-permute-start.14 = (bf16[2,64,512]{2,1,0:T(8,128)(2,1)}, bf16[2,64,512]{2,1,0:T(8,128)(2,1)S(1)}, u32[]{:S(2)}, u32[]{:S(2)}) collective-permute-start(bf16[2,64,512]{2,1,0:T(8,128)(2,1)} %get-tuple-element.33), channel_id=1, source_target_pairs={{0,480},{32,0},{64,32},{96,64},{128,96},{160,128},{192,160},{224,1... | collective-permute-start | bytes 393224 | tf_op jit(solution)/shard_map/ppermute | solution.py:138
  239.4 1.3 copy-start.2
  267.0 0.6 copy-start.9
  267.0 0.7 copy-start.10
  267.0 0.7 copy-start.11
  267.1 0.7 copy-start.12
  267.8 0.7 copy-start.13

commit v3 on v2

v3 whole, which is shorter than its diff:
```python
import functools
import math

import jax
import jax.numpy as jnp
from jax import lax
from jax.experimental import pallas as pl
from jax.experimental.pallas import tpu as pltpu
from jax.sharding import Mesh
from jax.sharding import PartitionSpec as P


D = 1024
F = 512
ITERS = 5
GROUP = ("group_0", "group_1", "group_2")

coefficients = (3.4445, -4.775, 2.0315)
momentum_decay = 0.95
learning_rate = 0.05
clip_rms = 0.5

FAR = (8, 7, 9, 6, 10)
NEAR = (5, 11, 4, 12, 3, 13, 2, 14, 1, 15)
LATE = (3, 13, 2, 14, 1, 15)


def squares_kernel(gradient_ref, out_ref, sum_ref):
    step = pl.program_id(0)
    widened = gradient_ref[...].astype(jnp.float32)
    part = jnp.sum((widened * widened).reshape(-1, 8, F), axis=0)

    @pl.when(step == 0)
    def _():
        sum_ref[...] = part

    @pl.when(step > 0)
    def _():
        sum_ref[...] += part

    @pl.when(step == pl.num_programs(0) - 1)
    def _():
        out_ref[...] = jnp.full(out_ref.shape, jnp.sum(sum_ref[...]), jnp.float32)


def sum_of_squares(x, copies):
    flat = x.reshape(-1, F)
    steps = 4
    return pl.pallas_call(
        squares_kernel,
        grid=(steps,),
        in_specs=[pl.BlockSpec((flat.shape[0] // steps, F), lambda i: (i, 0))],
        out_specs=pl.BlockSpec((copies, 8, 128), lambda i: (0, 0, 0)),
        out_shape=jax.ShapeDtypeStruct((copies, 8, 128), jnp.float32),
        scratch_shapes=[pltpu.VMEM((8, F), jnp.float32)],
    )(flat)


def add_kernel(parts_ref, out_ref):
    out_ref[...] = jnp.broadcast_to(jnp.sum(parts_ref[...], axis=0)[None], out_ref.shape)


def added(parts, copies):
    vmem = pl.BlockSpec(memory_space=pltpu.VMEM)
    return pl.pallas_call(
        add_kernel,
        in_specs=[vmem],
        out_specs=vmem,
        out_shape=jax.ShapeDtypeStruct((copies, 8, 128), jnp.float32),
    )(parts)


def everyone(x, axes):
    return lax.all_to_all(x, axes, split_axis=0, concat_axis=0, tiled=True)


def orthogonal_kernel(state_ref, prompt_ref, out_ref, iterate_ref):
    rows = iterate_ref.shape[0]
    widened = state_ref[...].reshape(rows, F).astype(jnp.float32)
    inverse_norm = 1.0 / (jnp.sqrt(jnp.sum(widened * widened)) + 1e-07)
    iterate_ref[...] = (widened * inverse_norm).astype(jnp.bfloat16)

    def iteration(_, carry):
        iterate = iterate_ref[...]
        gram = lax.dot_general(
            iterate, iterate, (((0,), (0,)), ((), ())), preferred_element_type=jnp.float32
        ).astype(jnp.bfloat16)
        squared = jnp.dot(gram, gram, preferred_element_type=jnp.float32)
        polynomial = (
            coefficients[1] * gram.astype(jnp.float32) + coefficients[2] * squared
        ).astype(jnp.bfloat16)
        product = jnp.dot(iterate, polynomial, preferred_element_type=jnp.float32)
        iterate_ref[...] = (coefficients[0] * iterate.astype(jnp.float32) + product).astype(
            jnp.bfloat16
        )
        return carry

    lax.fori_loop(0, ITERS, iteration, 0)
    update = (0.2 * math.sqrt(D) * iterate_ref[...].astype(jnp.float32)).astype(jnp.bfloat16)
    product = jnp.dot(prompt_ref[...], update, preferred_element_type=jnp.float32)
    out_ref[0] = -learning_rate * product


def orthogonal(states, prompt):
    shards, matrices, rows, _ = states.shape
    count = prompt.shape[0]
    return pl.pallas_call(
        orthogonal_kernel,
        grid=(matrices,),
        in_specs=[
            pl.BlockSpec((shards, 1, rows, F), lambda k: (0, k, 0, 0)),
            pl.BlockSpec(prompt.shape, lambda k: (0, 0)),
        ],
        out_specs=pl.BlockSpec((1, count, F), lambda k: (k, 0, 0)),
        out_shape=jax.ShapeDtypeStruct((matrices, count, F), jnp.float32),
        scratch_shapes=[pltpu.VMEM((shards * rows, F), jnp.bfloat16)],
        cost_estimate=pl.CostEstimate(flops=14_000_000_000, transcendentals=0, bytes_accessed=4 << 20),
    )(states, prompt)


def pick_kernel(distances, shards, slots_ref, position_ref, weights_ref, *refs):
    *out_refs, semaphores = refs
    copies = []
    for k, distance in enumerate(distances):
        slot = lax.rem(position_ref[0] + distance, shards)
        copies.append(
            pltpu.make_async_copy(weights_ref.at[slots_ref[slot]], out_refs[k], semaphores.at[k])
        )
    for copy in copies:
        copy.start()
    for copy in copies:
        copy.wait()


def picked_by_distance(slots, position, paired, distances):
    smem = pl.BlockSpec(memory_space=pltpu.SMEM)
    vmem = pl.BlockSpec(memory_space=pltpu.VMEM)
    blocks = pl.pallas_call(
        functools.partial(pick_kernel, distances, slots.shape[0]),
        in_specs=[smem, smem, pl.BlockSpec(memory_space=pl.ANY)],
        out_specs=[vmem] * len(distances),
        out_shape=[jax.ShapeDtypeStruct(paired.shape[1:], paired.dtype)] * len(distances),
        scratch_shapes=[pltpu.SemaphoreType.DMA((len(distances),))],
    )(slots, position, paired)
    return dict(zip(distances, blocks, strict=True))


def add_blocks(position, distances, blocks, prompt_ref, sums_ref):
    shards = prompt_ref.shape[0]
    outs = [sums_ref[0], sums_ref[1]]
    for distance, block in zip(distances, blocks, strict=True):
        part = prompt_ref[lax.rem(position + (shards - distance), shards)]
        for k in range(2):
            outs[k] += jnp.dot(part, block[k], preferred_element_type=jnp.float32)
    return outs


def early_kernel(distances, position_ref, prompt_ref, sums_ref, *refs):
    *blocks, out_ref = refs
    gate, up = add_blocks(position_ref[0], distances, blocks, prompt_ref, sums_ref)
    out_ref[0] = gate
    out_ref[1] = up


def late_kernel(distances, position_ref, prompt_ref, sums_ref, *refs):
    *blocks, out_ref = refs
    gate, up = add_blocks(position_ref[0], distances, blocks, prompt_ref, sums_ref)
    out_ref[...] = (gate / (1.0 + jnp.exp(-gate)) * up).astype(jnp.bfloat16)


def step_and_prefill(momentum, gradient, weights, slot_map, tokens):
    shards = lax.axis_size("shard")
    every_entry = shards * lax.axis_size(GROUP) * D * F
    rows = weights.shape[1]
    position = lax.axis_index("shard")
    slots = slot_map[0]
    paired = weights.reshape(shards // 2, 2, rows, F)

    at = position.reshape(1).astype(jnp.int32)
    mine = picked_by_distance(slots, at, paired, FAR)
    mine |= picked_by_distance(slots, at, paired, (0, *NEAR))
    old = {0: mine[0]}
    for distance in (*FAR, *NEAR):
        old[distance] = lax.ppermute(
            mine[distance], "shard", [(k, (k + distance) % shards) for k in range(shards)]
        )

    squares = sum_of_squares(gradient, shards)
    parts = everyone(squares, "shard")
    parts = added(parts, lax.axis_size(GROUP))
    parts = everyone(parts, GROUP)
    grand_total = jnp.sum(parts[:, 0, 0])
    widened = gradient.astype(jnp.float32)
    clip_factor = jnp.minimum(
        1.0, clip_rms * math.sqrt(every_entry) / jnp.sqrt(grand_total + 1e-06)
    )
    fresh_state = (momentum_decay * momentum.astype(jnp.float32) + clip_factor * widened).astype(
        jnp.bfloat16
    )
    picked = fresh_state.reshape(paired.shape).at[slots].get(mode="promise_in_bounds")
    states = lax.all_to_all(picked, "shard", split_axis=0, concat_axis=0, tiled=True)
    sums = orthogonal(states, tokens[0, 0])

    prompt = jnp.moveaxis(tokens[0, 0].reshape(-1, shards, rows), 1, 0)
    early = tuple(d for d in old if d not in LATE)
    smem = pl.BlockSpec(memory_space=pltpu.SMEM)
    vmem = pl.BlockSpec(memory_space=pltpu.VMEM)
    count = prompt.shape[1]
    sums = pl.pallas_call(
        functools.partial(early_kernel, early),
        in_specs=[smem] + [vmem] * (2 + len(early)),
        out_specs=vmem,
        out_shape=jax.ShapeDtypeStruct((2, count, F), jnp.float32),
    )(at, prompt, sums, *(old[d] for d in early))
    hidden = pl.pallas_call(
        functools.partial(late_kernel, LATE),
        in_specs=[smem] + [vmem] * (2 + len(LATE)),
        out_specs=vmem,
        out_shape=jax.ShapeDtypeStruct((count, F), jnp.bfloat16),
    )(at, prompt, sums, *(old[d] for d in LATE))
    return (fresh_state, hidden[None, None])


def solution(mesh):
    split = Mesh(
        mesh.devices.reshape(mesh.shape["shard"], 4, 4, 2),
        ("shard", "group_0", "group_1", "group_2"),
    )
    placed = (
        P(GROUP, "shard", None),
        P(GROUP, "shard", None),
        P(GROUP, "shard", None),
        P(GROUP, None),
        P("shard", GROUP, None, None),
    )
    return jax.shard_map(
        step_and_prefill,
        mesh=split,
        in_specs=placed,
        out_specs=(P(GROUP, "shard", None), P("shard", GROUP, None, None)),
        check_vma=False,
    )
```

time: 273 us -> 273 us (level)
  Pallas kernels: 33 us -> 40.4 us
  waiting for transfers between devices: 95.9 us -> 92.4 us
  other arithmetic: 5.98 us -> 2.92 us
    pallas_call x1 -> x4, Pallas kernels: 2.68 us -> 10.6 us  [the longest x2 6.15 us: picked_by_distance(): pl.pallas_call(functools.partial(pick_kernel, distances, slots.shape[0]),...]
    ppermute x15, waiting for transfers between devices: 88.7 us -> 85.2 us  [step_and_prefill(): lax.ppermute(mine[distance], 'shard', [(k, (k + distance) % shards) for k...]
    reduce_sum x3 -> x1, other arithmetic: 3.71 us -> 0.63 us  [step_and_prefill(): grand_total = jnp.sum(parts[:, 0, 0])]
  transfers between devices with their start and end apart: 17 -> 17, of which waited for: 4 -> 4; matrix products, arithmetic and copies ran while one was open for 1% -> 1% of each run, Pallas kernels for 11% -> 12%
where the time goes in v3:
time: 273 us; the launch traced here: 272 us
  starting transfers between devices  101 us (37%)
  waiting for transfers between devices  92.4 us (34%)
  Pallas kernels  40.4 us (15%)
  blocking collectives  26.8 us (10%)
  local copies, waits for them, and re-layouts  7 us (3%)
  other arithmetic  2.92 us (1%)
    ppermute x15, starting transfers between devices, step_and_prefill(): lax.ppermute(mine[distance], 'shard', [(k, (k + distance) % shards) for k...  88.4 us
    ppermute x15, waiting for transfers between devices, step_and_prefill(): lax.ppermute(mine[distance], 'shard', [(k, (k + distance) % shards) for k...  85.2 us
    all_to_all x1, blocking collectives, everyone(): return lax.all_to_all(x, axes, split_axis=0, concat_axis=0, tiled=True)  26.8 us
    pallas_call x1, Pallas kernels, orthogonal(): pl.pallas_call(orthogonal_kernel, grid=(matrices,), in_specs=[pl.BlockSpe...  22.1 us
    all_to_all x1, starting transfers between devices, everyone(): return lax.all_to_all(x, axes, split_axis=0, concat_axis=0, tiled=True)  7.32 us
    all_to_all x1, waiting for transfers between devices, everyone(): return lax.all_to_all(x, axes, split_axis=0, concat_axis=0, tiled=True)  7.16 us
    pallas_call x2, Pallas kernels, picked_by_distance(): pl.pallas_call(functools.partial(pick_kernel, distances, slots.shape[0]),...  6.15 us
  transfers between devices with their start and end apart: 17, of which 4 were waited for; matrix products, arithmetic and copies ran while one was open for 1% of the time, Pallas kernels for 12%

profile of v3, /device:TPU:32, one launch (start us, length us, event | category | flops | bytes accessed | tf_op | source)
XLA Modules:
  0.0 271.7 jit_solution(5040470889800579229)
XLA Ops:
  0.6 2.9 %shard_map.68 = f32[16,8,128]{2,1,0:T(8,128)} custom-call(bf16[1024,512]{1,0:T(8,128)(2,1)} %bitcast.18), custom_call_target="tpu_custom_call" | custom-call | tf_op jit(solution)/shard_map/pallas_call | solution.py:49
  3.6 26.8 %all_to_all.15.parts_ref = f32[16,8,128]{2,1,0:T(8,128)} all-to-all(f32[16,8,128]{2,1,0:T(8,128)} %shard_map.68), channel_id=1, replica_groups=mesh['shard'=16,'group_0'=4,'group_1'=4,'group_2'=2] {'shard'}, dimensions={0} | all-to-all | bytes 131072 | tf_op jit(solution)/shard_map/all_to_all | solution.py:74
  30.4 1.5 shard_map.69
  31.9 7.3 %all-to-all-start.1 = ((f32[32,8,128]{2,1,0:T(8,128)}), f32[32,8,128]{2,1,0:T(8,128)S(1)}, u32[]{:S(2)}, u32[]{:S(2)}) async-start(f32[32,8,128]{2,1,0:T(8,128)} %shard_map.69), calls=%async_computation.1 | async-start | bytes 262144 | tf_op jit(solution)/shard_map/all_to_all | solution.py:74
  39.2 0.7 fusion
  39.9 7.2 %all-to-all-done.1 = f32[32,8,128]{2,1,0:T(8,128)S(1)} async-done(((f32[32,8,128]{2,1,0:T(8,128)}), f32[32,8,128]{2,1,0:T(8,128)S(1)}, u32[]{:S(2)}, u32[]{:S(2)}) %all-to-all-start.1) | async-done | bytes 131104 | tf_op jit(solution)/shard_map/all_to_all | solution.py:74
  47.1 0.6 slice_reduce_fusion
  48.4 1.6 add_convert_fusion
  50.0 0.0 copy-start
  50.1 2.0 gather_fusion
  52.1 4.8 %all-to-all-start.2 = ((bf16[16,2,64,512]{3,2,1,0:T(8,128)(2,1)}), bf16[16,2,64,512]{3,2,1,0:T(8,128)(2,1)S(1)}, u32[]{:S(2)}, u32[]{:S(2)}) async-start(bf16[16,2,64,512]{3,2,1,0:T(8,128)(2,1)} %gather_fusion), calls=%async_computation.2 | async-start | bytes 4194304 | tf_op jit(solution)/shard_map/all_to_all | solution.py:201
  56.9 2.9 %shard_map.72 = (bf16[2,64,512]{2,1,0:T(8,128)(2,1)}, bf16[2,64,512]{2,1,0:T(8,128)(2,1)}, bf16[2,64,512]{2,1,0:T(8,128)(2,1)}, bf16[2,64,512]{2,1,0:T(8,128)(2,1)}, bf16[2,64,512]{2,1,0:T(8,128)(2,1)}) custom-call(s32[16]{0:T(128)} %bitcast.22, s32[1]{0:T(128)} %bitcast.1.position_ref, bf16[8,2,64,512]{3,2,1,0:T(8,128)(2,1)} %bitcast.16), custom_call_target="tpu_custom_call" | custom-call | tf_op jit(solution)/shard_map/pallas_call | solution.py:138
  59.8 11.2 %collective-permute-start = (bf16[2,64,512]{2,1,0:T(8,128)(2,1)}, bf16[2,64,512]{2,1,0:T(8,128)(2,1)S(1)}, u32[]{:S(2)}, u32[]{:S(2)}) collective-permute-start(bf16[2,64,512]{2,1,0:T(8,128)(2,1)} %get-tuple-element.19), channel_id=1, source_target_pairs={{0,256},{32,288},{64,320},{96,352},{128,384},{160,416},{192,448},{... | collective-permute-start | bytes 393224 | tf_op jit(solution)/shard_map/ppermute | solution.py:184
  71.0 2.1 collective-permute-start.1
  73.1 11.6 %collective-permute-start.2 = (bf16[2,64,512]{2,1,0:T(8,128)(2,1)}, bf16[2,64,512]{2,1,0:T(8,128)(2,1)S(1)}, u32[]{:S(2)}, u32[]{:S(2)}) collective-permute-start(bf16[2,64,512]{2,1,0:T(8,128)(2,1)} %get-tuple-element.21), channel_id=1, source_target_pairs={{0,288},{32,320},{64,352},{96,384},{128,416},{160,448},{192,480},{... | collective-permute-start | bytes 393224 | tf_op jit(solution)/shard_map/ppermute | solution.py:184
  84.7 1.9 collective-permute-start.3
  86.6 10.8 %collective-permute-start.4 = (bf16[2,64,512]{2,1,0:T(8,128)(2,1)}, bf16[2,64,512]{2,1,0:T(8,128)(2,1)S(1)}, u32[]{:S(2)}, u32[]{:S(2)}) collective-permute-start(bf16[2,64,512]{2,1,0:T(8,128)(2,1)} %get-tuple-element.23), channel_id=1, source_target_pairs={{0,320},{32,352},{64,384},{96,416},{128,448},{160,480},{192,0},{22... | collective-permute-start | bytes 393224 | tf_op jit(solution)/shard_map/ppermute | solution.py:184
  97.5 3.3 %shard_map.71 = (bf16[2,64,512]{2,1,0:T(8,128)(2,1)}, bf16[2,64,512]{2,1,0:T(8,128)(2,1)}, bf16[2,64,512]{2,1,0:T(8,128)(2,1)}, bf16[2,64,512]{2,1,0:T(8,128)(2,...) custom-call(s32[16]{0:T(128)} %bitcast.23, ...), custom_call_target="tpu_custom_call" | custom-call | tf_op jit(solution)/shard_map/pallas_call | solution.py:138
  100.8 67.3 %collective-permute-done.refs_1_ = bf16[2,64,512]{2,1,0:T(8,128)(2,1)S(1)} collective-permute-done((bf16[2,64,512]{2,1,0:T(8,128)(2,1)}, bf16[2,64,512]{2,1,0:T(8,128)(2,1)S(1)}, u32[]{:S(2)}, u32[]{:S(2)}) %collective-permute-start) | collective-permute-done | bytes 131104 | tf_op jit(solution)/shard_map/ppermute | solution.py:184
  168.0 6.9 %collective-permute-start.5 = (bf16[2,64,512]{2,1,0:T(8,128)(2,1)}, bf16[2,64,512]{2,1,0:T(8,128)(2,1)}, u32[]{:S(2)}, u32[]{:S(2)}) collective-permute-start(bf16[2,64,512]{2,1,0:T(8,128)(2,1)} %get-tuple-element.24), channel_id=1, source_target_pairs={{0,160},{32,192},{64,224},{96,256},{128,288},{160,320},{192,352},{... | collective-permute-start | bytes 393224 | tf_op jit(solution)/shard_map/ppermute | solution.py:184
  175.0 10.7 %collective-permute-done.1.refs_2_ = bf16[2,64,512]{2,1,0:T(8,128)(2,1)S(1)} collective-permute-done((bf16[2,64,512]{2,1,0:T(8,128)(2,1)}, bf16[2,64,512]{2,1,0:T(8,128)(2,1)S(1)}, u32[]{:S(2)}, u32[]{:S(2)}) %collective-permute-start.1) | collective-permute-done | bytes 131104 | tf_op jit(solution)/shard_map/ppermute | solution.py:184
  185.7 9.2 %collective-permute-start.6 = (bf16[2,64,512]{2,1,0:T(8,128)(2,1)}, bf16[2,64,512]{2,1,0:T(8,128)(2,1)}, u32[]{:S(2)}, u32[]{:S(2)}) collective-permute-start(bf16[2,64,512]{2,1,0:T(8,128)(2,1)} %get-tuple-element.25), channel_id=1, source_target_pairs={{0,352},{32,384},{64,416},{96,448},{128,480},{160,0},{192,32},{224... | collective-permute-start | bytes 393224 | tf_op jit(solution)/shard_map/ppermute | solution.py:184
  194.9 0.0 collective-permute-done.2.refs_3_
  194.9 2.3 collective-permute-start.7
  197.2 7.2 %collective-permute-done.3.refs_4_ = bf16[2,64,512]{2,1,0:T(8,128)(2,1)S(1)} collective-permute-done((bf16[2,64,512]{2,1,0:T(8,128)(2,1)}, bf16[2,64,512]{2,1,0:T(8,128)(2,1)S(1)}, u32[]{:S(2)}, u32[]{:S(2)}) %collective-permute-start.3) | collective-permute-done | bytes 131104 | tf_op jit(solution)/shard_map/ppermute | solution.py:184
  204.4 2.0 collective-permute-start.8
  206.4 0.0 collective-permute-done.4.refs_5_
  206.5 0.6 copy-done.8
  207.1 11.7 %collective-permute-start.9 = (bf16[2,64,512]{2,1,0:T(8,128)(2,1)}, bf16[2,64,512]{2,1,0:T(8,128)(2,1)}, u32[]{:S(2)}, u32[]{:S(2)}) collective-permute-start(bf16[2,64,512]{2,1,0:T(8,128)(2,1)} %get-tuple-element.28), channel_id=1, source_target_pairs={{0,96},{32,128},{64,160},{96,192},{128,224},{160,256},{192,288},{2... | collective-permute-start | bytes 393224 | tf_op jit(solution)/shard_map/ppermute | solution.py:184
  218.8 0.2 copy.7
  219.0 1.3 copy.8
  220.4 0.0 collective-permute-done.5.refs_6_
  220.4 1.9 collective-permute-start.10
  222.3 0.0 collective-permute-done.6.refs_7_
  222.3 6.1 %collective-permute-start.11 = (bf16[2,64,512]{2,1,0:T(8,128)(2,1)}, bf16[2,64,512]{2,1,0:T(8,128)(2,1)S(1)}, u32[]{:S(2)}, u32[]{:S(2)}) collective-permute-start(bf16[2,64,512]{2,1,0:T(8,128)(2,1)} %get-tuple-element.30), channel_id=1, source_target_pairs={{0,64},{32,96},{64,128},{96,160},{128,192},{160,224},{192,256},{22... | collective-permute-start | bytes 393224 | tf_op jit(solution)/shard_map/ppermute | solution.py:184
  228.4 3.0 %collective-permute-start.12 = (bf16[2,64,512]{2,1,0:T(8,128)(2,1)}, bf16[2,64,512]{2,1,0:T(8,128)(2,1)S(1)}, u32[]{:S(2)}, u32[]{:S(2)}) collective-permute-start(bf16[2,64,512]{2,1,0:T(8,128)(2,1)} %get-tuple-element.31), channel_id=1, source_target_pairs={{0,448},{32,480},{64,0},{96,32},{128,64},{160,96},{192,128},{224,1... | collective-permute-start | bytes 393224 | tf_op jit(solution)/shard_map/ppermute | solution.py:184
  231.5 4.3 %collective-permute-start.13 = (bf16[2,64,512]{2,1,0:T(8,128)(2,1)}, bf16[2,64,512]{2,1,0:T(8,128)(2,1)S(1)}, u32[]{:S(2)}, u32[]{:S(2)}) collective-permute-start(bf16[2,64,512]{2,1,0:T(8,128)(2,1)} %get-tuple-element.32), channel_id=1, source_target_pairs={{0,32},{32,64},{64,96},{96,128},{128,160},{160,192},{192,224},{224... | collective-permute-start | bytes 393224 | tf_op jit(solution)/shard_map/ppermute | solution.py:184
  235.8 0.0 collective-permute-done.9.refs_0_
  235.8 3.2 %collective-permute-start.14 = (bf16[2,64,512]{2,1,0:T(8,128)(2,1)}, bf16[2,64,512]{2,1,0:T(8,128)(2,1)S(1)}, u32[]{:S(2)}, u32[]{:S(2)}) collective-permute-start(bf16[2,64,512]{2,1,0:T(8,128)(2,1)} %get-tuple-element.33), channel_id=1, source_target_pairs={{0,480},{32,0},{64,32},{96,64},{128,96},{160,128},{192,160},{224,1... | collective-permute-start | bytes 393224 | tf_op jit(solution)/shard_map/ppermute | solution.py:184
  239.0 1.4 copy-done.2
  240.4 22.1 %shard_map.70.sums_ref = f32[2,256,512]{2,1,0:T(8,128)} custom-call(bf16[16,2,64,512]{3,2,1,0:T(8,128)(2,1)} %copy-done.2, bf16[256,1024]{1,0:T(8,128)(2,1)} %bitcast.20), custom_call_target="tpu_custom_call" | custom-call | flops 14000000000 | bytes 4194304 | tf_op jit(solution)/shard_map/pallas_call | solution.py:107
  262.5 4.4 %shard_map.73.sums_ref = f32[2,256,512]{2,1,0:T(8,128)} custom-call(s32[1]{0:T(128)} %bitcast.1.position_ref, bf16[16,256,64]{2,1,0:T(8,128)(2,1)} %bitcast.13, f32[2,256,512]{2,1,0:T(8,128)} %shard_map.70.sums_ref, bf16[2,64,512]{2,1,0:T(8,128)(2,1)} %get-tuple-element.18.refs_0_, bf16[2,64,512]{2,1,0:T(8,128)(2,1)} %copy-done.4, ...), custom_call_target="tpu_custom_call" | custom-call | tf_op jit(solution)/shard_map/pallas_call | solution.py:209
  266.9 0.6 copy-done.9
  267.5 0.0 copy-done.10
  267.5 0.1 copy-done.11
  267.6 0.1 copy-done.12
  267.7 0.6 copy-done.13
  268.3 3.4 %shard_map.74 = bf16[256,512]{1,0:T(8,128)(2,1)} custom-call(s32[1]{0:T(128)} %bitcast.1.position_ref, bf16[16,256,64]{2,1,0:T(8,128)(2,1)} %bitcast.14, f32[2,256,512]{2,1,0:T(8,128)} %shard_map.73.sums_ref, bf16[2,64,512]{2,1,0:T(8,128)(2,1)} %collective-permute-done.9.refs_0_, bf16[2,64,512]{2,1,0:T(8,128)(2,1)} %copy-done.9, ...), custom_call_target="tpu_custom_call" | custom-call | tf_op jit(solution)/shard_map/pallas_call | solution.py:215
  (29 shorter events, 0.1 us)
Async XLA Ops:
  0.6 47.8 %copy-start.1 = (bf16[16,64,512]{2,1,0:T(8,128)(2,1)S(1)}, bf16[16,64,512]{2,1,0:T(8,128)(2,1)}, u32[]{:S(2)}) copy-start(bf16[16,64,512]{2,1,0:T(8,128)(2,1)} %param.6) | copy-start | bytes 3145732
  31.9 15.2 %all-to-all-start.1 = ((f32[32,8,128]{2,1,0:T(8,128)}), f32[32,8,128]{2,1,0:T(8,128)S(1)}, u32[]{:S(2)}, u32[]{:S(2)}) async-start(f32[32,8,128]{2,1,0:T(8,128)} %shard_map.69), calls=%async_computation.1 | async-start | bytes 262144 | tf_op jit(solution)/shard_map/all_to_all | solution.py:74
  50.0 2.1 copy-start
  52.1 186.9 %all-to-all-start.2 = ((bf16[16,2,64,512]{3,2,1,0:T(8,128)(2,1)}), bf16[16,2,64,512]{3,2,1,0:T(8,128)(2,1)S(1)}, u32[]{:S(2)}, u32[]{:S(2)}) async-start(bf16[16,2,64,512]{3,2,1,0:T(8,128)(2,1)} %gather_fusion), calls=%async_computation.2 | async-start | bytes 4194304 | tf_op jit(solution)/shard_map/all_to_all | solution.py:201
  56.9 161.9 %copy-start.3 = (bf16[1,1,256,1024]{3,2,1,0:T(8,128)(2,1)S(1)}, bf16[1,1,256,1024]{3,2,1,0:T(8,128)(2,1)}, u32[]{:S(2)}) copy-start(bf16[1,1,256,1024]{3,2,1,0:T(8,128)(2,1)} %param.9) | copy-start | bytes 1572868
  59.8 108.2 %collective-permute-start = (bf16[2,64,512]{2,1,0:T(8,128)(2,1)}, bf16[2,64,512]{2,1,0:T(8,128)(2,1)S(1)}, u32[]{:S(2)}, u32[]{:S(2)}) collective-permute-start(bf16[2,64,512]{2,1,0:T(8,128)(2,1)} %get-tuple-element.19), channel_id=1, source_target_pairs={{0,256},{32,288},{64,320},{96,352},{128,384},{160,416},{192,448},{... | collective-permute-start | bytes 393224 | tf_op jit(solution)/shard_map/ppermute | solution.py:184
  71.0 114.6 %collective-permute-start.1 = (bf16[2,64,512]{2,1,0:T(8,128)(2,1)}, bf16[2,64,512]{2,1,0:T(8,128)(2,1)S(1)}, u32[]{:S(2)}, u32[]{:S(2)}) collective-permute-start(bf16[2,64,512]{2,1,0:T(8,128)(2,1)} %get-tuple-element.20), channel_id=1, source_target_pairs={{0,224},{32,256},{64,288},{96,320},{128,352},{160,384},{192,416},{... | collective-permute-start | bytes 393224 | tf_op jit(solution)/shard_map/ppermute | solution.py:184
  73.1 121.8 %collective-permute-start.2 = (bf16[2,64,512]{2,1,0:T(8,128)(2,1)}, bf16[2,64,512]{2,1,0:T(8,128)(2,1)S(1)}, u32[]{:S(2)}, u32[]{:S(2)}) collective-permute-start(bf16[2,64,512]{2,1,0:T(8,128)(2,1)} %get-tuple-element.21), channel_id=1, source_target_pairs={{0,288},{32,320},{64,352},{96,384},{128,416},{160,448},{192,480},{... | collective-permute-start | bytes 393224 | tf_op jit(solution)/shard_map/ppermute | solution.py:184
  84.7 119.7 %collective-permute-start.3 = (bf16[2,64,512]{2,1,0:T(8,128)(2,1)}, bf16[2,64,512]{2,1,0:T(8,128)(2,1)S(1)}, u32[]{:S(2)}, u32[]{:S(2)}) collective-permute-start(bf16[2,64,512]{2,1,0:T(8,128)(2,1)} %get-tuple-element.22), channel_id=1, source_target_pairs={{0,192},{32,224},{64,256},{96,288},{128,320},{160,352},{192,384},{... | collective-permute-start | bytes 393224 | tf_op jit(solution)/shard_map/ppermute | solution.py:184
  86.6 119.8 %collective-permute-start.4 = (bf16[2,64,512]{2,1,0:T(8,128)(2,1)}, bf16[2,64,512]{2,1,0:T(8,128)(2,1)S(1)}, u32[]{:S(2)}, u32[]{:S(2)}) collective-permute-start(bf16[2,64,512]{2,1,0:T(8,128)(2,1)} %get-tuple-element.23), channel_id=1, source_target_pairs={{0,320},{32,352},{64,384},{96,416},{128,448},{160,480},{192,0},{22... | collective-permute-start | bytes 393224 | tf_op jit(solution)/shard_map/ppermute | solution.py:184
  168.0 94.4 %copy-start.4 = (bf16[2,64,512]{2,1,0:T(8,128)(2,1)}, bf16[2,64,512]{2,1,0:T(8,128)(2,1)S(1)}, u32[]{:S(2)}) copy-start(bf16[2,64,512]{2,1,0:T(8,128)(2,1)S(1)} %collective-permute-done.refs_1_) | copy-start | bytes 393220
  168.0 52.3 %collective-permute-start.5 = (bf16[2,64,512]{2,1,0:T(8,128)(2,1)}, bf16[2,64,512]{2,1,0:T(8,128)(2,1)}, u32[]{:S(2)}, u32[]{:S(2)}) collective-permute-start(bf16[2,64,512]{2,1,0:T(8,128)(2,1)} %get-tuple-element.24), channel_id=1, source_target_pairs={{0,160},{32,192},{64,224},{96,256},{128,288},{160,320},{192,352},{... | collective-permute-start | bytes 393224 | tf_op jit(solution)/shard_map/ppermute | solution.py:184
  185.7 76.8 %copy-start.5 = (bf16[2,64,512]{2,1,0:T(8,128)(2,1)}, bf16[2,64,512]{2,1,0:T(8,128)(2,1)S(1)}, u32[]{:S(2)}) copy-start(bf16[2,64,512]{2,1,0:T(8,128)(2,1)S(1)} %collective-permute-done.1.refs_2_) | copy-start | bytes 393220
  185.7 36.6 %collective-permute-start.6 = (bf16[2,64,512]{2,1,0:T(8,128)(2,1)}, bf16[2,64,512]{2,1,0:T(8,128)(2,1)}, u32[]{:S(2)}, u32[]{:S(2)}) collective-permute-start(bf16[2,64,512]{2,1,0:T(8,128)(2,1)} %get-tuple-element.25), channel_id=1, source_target_pairs={{0,352},{32,384},{64,416},{96,448},{128,480},{160,0},{192,32},{224... | collective-permute-start | bytes 393224 | tf_op jit(solution)/shard_map/ppermute | solution.py:184
  194.9 67.6 %copy-start.6 = (bf16[2,64,512]{2,1,0:T(8,128)(2,1)}, bf16[2,64,512]{2,1,0:T(8,128)(2,1)S(1)}, u32[]{:S(2)}) copy-start(bf16[2,64,512]{2,1,0:T(8,128)(2,1)S(1)} %collective-permute-done.2.refs_3_) | copy-start | bytes 393220
  194.9 33.5 %collective-permute-start.7 = (bf16[2,64,512]{2,1,0:T(8,128)(2,1)}, bf16[2,64,512]{2,1,0:T(8,128)(2,1)}, u32[]{:S(2)}, u32[]{:S(2)}) collective-permute-start(bf16[2,64,512]{2,1,0:T(8,128)(2,1)} %get-tuple-element.26), channel_id=1, source_target_pairs={{0,128},{32,160},{64,192},{96,224},{128,256},{160,288},{192,320},{... | collective-permute-start | bytes 393224 | tf_op jit(solution)/shard_map/ppermute | solution.py:184
  204.4 2.0 copy-start.7
  204.4 27.0 %collective-permute-start.8 = (bf16[2,64,512]{2,1,0:T(8,128)(2,1)}, bf16[2,64,512]{2,1,0:T(8,128)(2,1)}, u32[]{:S(2)}, u32[]{:S(2)}) collective-permute-start(bf16[2,64,512]{2,1,0:T(8,128)(2,1)} %get-tuple-element.27), channel_id=1, source_target_pairs={{0,384},{32,416},{64,448},{96,480},{128,0},{160,32},{192,64},{224,... | collective-permute-start | bytes 393224 | tf_op jit(solution)/shard_map/ppermute | solution.py:184
  206.4 0.7 copy-start.8
  207.1 28.7 %collective-permute-start.9 = (bf16[2,64,512]{2,1,0:T(8,128)(2,1)}, bf16[2,64,512]{2,1,0:T(8,128)(2,1)}, u32[]{:S(2)}, u32[]{:S(2)}) collective-permute-start(bf16[2,64,512]{2,1,0:T(8,128)(2,1)} %get-tuple-element.28), channel_id=1, source_target_pairs={{0,96},{32,128},{64,160},{96,192},{128,224},{160,256},{192,288},{2... | collective-permute-start | bytes 393224 | tf_op jit(solution)/shard_map/ppermute | solution.py:184
  220.4 46.5 %collective-permute-start.10 = (bf16[2,64,512]{2,1,0:T(8,128)(2,1)}, bf16[2,64,512]{2,1,0:T(8,128)(2,1)S(1)}, u32[]{:S(2)}, u32[]{:S(2)}) collective-permute-start(bf16[2,64,512]{2,1,0:T(8,128)(2,1)} %get-tuple-element.29), channel_id=1, source_target_pairs={{0,416},{32,448},{64,480},{96,0},{128,32},{160,64},{192,96},{224,1... | collective-permute-start | bytes 393224 | tf_op jit(solution)/shard_map/ppermute | solution.py:184
  222.3 44.6 %collective-permute-start.11 = (bf16[2,64,512]{2,1,0:T(8,128)(2,1)}, bf16[2,64,512]{2,1,0:T(8,128)(2,1)S(1)}, u32[]{:S(2)}, u32[]{:S(2)}) collective-permute-start(bf16[2,64,512]{2,1,0:T(8,128)(2,1)} %get-tuple-element.30), channel_id=1, source_target_pairs={{0,64},{32,96},{64,128},{96,160},{128,192},{160,224},{192,256},{22... | collective-permute-start | bytes 393224 | tf_op jit(solution)/shard_map/ppermute | solution.py:184
  228.4 38.4 %collective-permute-start.12 = (bf16[2,64,512]{2,1,0:T(8,128)(2,1)}, bf16[2,64,512]{2,1,0:T(8,128)(2,1)S(1)}, u32[]{:S(2)}, u32[]{:S(2)}) collective-permute-start(bf16[2,64,512]{2,1,0:T(8,128)(2,1)} %get-tuple-element.31), channel_id=1, source_target_pairs={{0,448},{32,480},{64,0},{96,32},{128,64},{160,96},{192,128},{224,1... | collective-permute-start | bytes 393224 | tf_op jit(solution)/shard_map/ppermute | solution.py:184
  231.5 35.4 %collective-permute-start.13 = (bf16[2,64,512]{2,1,0:T(8,128)(2,1)}, bf16[2,64,512]{2,1,0:T(8,128)(2,1)S(1)}, u32[]{:S(2)}, u32[]{:S(2)}) collective-permute-start(bf16[2,64,512]{2,1,0:T(8,128)(2,1)} %get-tuple-element.32), channel_id=1, source_target_pairs={{0,32},{32,64},{64,96},{96,128},{128,160},{160,192},{192,224},{224... | collective-permute-start | bytes 393224 | tf_op jit(solution)/shard_map/ppermute | solution.py:184
  235.8 31.1 %collective-permute-start.14 = (bf16[2,64,512]{2,1,0:T(8,128)(2,1)}, bf16[2,64,512]{2,1,0:T(8,128)(2,1)S(1)}, u32[]{:S(2)}, u32[]{:S(2)}) collective-permute-start(bf16[2,64,512]{2,1,0:T(8,128)(2,1)} %get-tuple-element.33), channel_id=1, source_target_pairs={{0,480},{32,0},{64,32},{96,64},{128,96},{160,128},{192,160},{224,1... | collective-permute-start | bytes 393224 | tf_op jit(solution)/shard_map/ppermute | solution.py:184
  239.0 1.4 copy-start.2
  266.8 0.6 copy-start.9
  266.8 0.7 copy-start.10
  266.9 0.7 copy-start.11
  266.9 0.8 copy-start.12
  267.7 0.6 copy-start.13
